TPU v7x, 256 devices: a whole 4x4x8 slice. The times are simulated.
256 devices in a mesh: dp: 8 (over y, core), owner: 32 (over x, z).
Axes of the slice: x: 4, y: 4, z: 8, core: 2. Of those that a mesh axis runs over, the one named last changes fastest.
Arguments:
- tokens: bfloat16 [32768, 8192], P(('dp', 'owner')), may hold values from -6 to 6
- adapter_index: int32 [32768, 1], P(('dp', 'owner')), may hold values from 0 to 63; in each aligned block of 128 rows (0 to 127, 128 to 255, ...) at most 3 rows name the same one
- query_cotangent: bfloat16 [32768, 8192], P(('dp', 'owner')), may hold values from -6 to 6
- value_cotangent: bfloat16 [32768, 1024], P(('dp', 'owner')), may hold values from -6 to 6
- shrink: bfloat16 [64, 2, 64, 8192], P('owner', None, None, 'dp'), may hold values from -0.0625 to 0.0625
- query_expand: bfloat16 [64, 64, 8192], P('owner', None, 'dp'), may hold values from -0.75 to 0.75
- value_expand: bfloat16 [64, 64, 1024], P('owner', None, 'dp'), may hold values from -0.75 to 0.75
Outputs:
- query_delta: bfloat16 [32768, 8192], P(('dp', 'owner'))
- value_delta: bfloat16 [32768, 1024], P(('dp', 'owner'))
- token_gradient: bfloat16 [32768, 8192], P(('dp', 'owner'))
- shrink_gradient: float32 [64, 2, 64, 8192], P('owner', None, None, 'dp')
- query_gradient: float32 [64, 64, 8192], P('owner', None, 'dp')
- value_gradient: float32 [64, 64, 1024], P('owner', None, 'dp')
Inputs may be any that keep to these rules, and one draw needn't show every extreme that they name: `adapter_index`: within each device's aligned block of 128 tokens no adapter is named by more than 3 tokens, a bound that some block reaches.
All inputs are finite; a program needn't handle non-finite values.
Results may differ from a plain program's by a relative error of at most 0.0049.
Values may be sent and summed in bfloat16 or wider, within the bound.
No kernel may reach another device: no remote copies, remote signals or barrier semaphores. Data moves between devices by JAX's collectives and lax.ppermute only.
A program may use at most 128 MiB of HBM per device.

v0:
```python
import jax
import jax.numpy as jnp
from jax import lax
from jax.experimental import pallas as pl
from jax.experimental.pallas import tpu as pltpu
from jax.sharding import Mesh, PartitionSpec as P

SCALE = 0.5
F32 = jnp.float32
BF16 = jnp.bfloat16
CAP = 3
TILE = 16
PER = 5
TILES = 3
GROUP = PER * TILES + 1
SLOTS = TILE * TILES


def iota(shape, dim):
    return lax.broadcasted_iota(jnp.int32, shape, dim)


def slot_of(adapter, ordinal):
    group = adapter >> 4
    inner = adapter & 15
    tile = (inner >= PER).astype(jnp.int32) + (inner >= 2 * PER).astype(jnp.int32)
    spot = jnp.where(
        inner == GROUP - 1, ordinal * TILE + TILE - 1, tile * TILE + (inner - tile * PER) * CAP + ordinal
    )
    return group * SLOTS + spot


def as_row(column):
    n = column.shape[0]
    return jnp.sum(jnp.where(iota((n, n), 0) == iota((n, n), 1), column, 0), axis=0, keepdims=True)


def placing_rows(adapter, slots):
    n = adapter.shape[0]
    row = as_row(adapter)
    same = (adapter == row) & (iota((n, n), 0) < iota((n, n), 1))
    target = slot_of(row, jnp.sum(same.astype(jnp.int32), axis=0, keepdims=True))
    return (iota((slots, n), 0) == target).astype(F32).astype(BF16)


def placing_columns(adapter, slots):
    n = adapter.shape[0]
    row = as_row(adapter)
    same = (adapter == row) & (iota((n, n), 1) < iota((n, n), 0))
    target = slot_of(adapter, jnp.sum(same.astype(jnp.int32), axis=1, keepdims=True))
    return (iota((n, slots), 1) == target).astype(F32).astype(BF16)


def row_block(rows):
    inner = iota((rows, 128), 0) & (TILE - 1)
    block = jnp.zeros((rows, 128), jnp.int32)
    for k in range(1, PER + 1):
        block = block + (inner >= CAP * k).astype(jnp.int32)
    return block


def pair_mask(rows, pair):
    half = (iota((rows, 128), 1) >= 64).astype(jnp.int32)
    return row_block(rows) == 2 * pair + half


def params():
    return pltpu.CompilerParams(vmem_limit_bytes=56 << 20)


def cost(flops, moved):
    return pl.CostEstimate(flops=flops, bytes_accessed=moved, transcendentals=0)


def place(adapter, values, parts, slots, name):
    n = adapter.shape[0]
    widths = [v.shape[1] // parts for v in values]
    total = sum(widths)

    def kernel(a_ref, *refs):
        ins, o_ref, p_ref = refs[: len(values)], refs[-2], refs[-1]

        @pl.when(pl.program_id(0) == 0)
        def _():
            p_ref[...] = placing_rows(a_ref[...], slots)

        at = 0
        for v_ref, width in zip(ins, widths):
            o_ref[0, :, at : at + width] = jnp.dot(
                p_ref[...], v_ref[...], preferred_element_type=F32
            ).astype(BF16)
            at += width

    return pl.pallas_call(
        kernel,
        grid=(parts,),
        in_specs=[pl.BlockSpec((n, 1), lambda j: (0, 0))]
        + [pl.BlockSpec((n, width), lambda j: (0, j)) for width in widths],
        out_specs=pl.BlockSpec((1, slots, total), lambda j: (j, 0, 0)),
        out_shape=jax.ShapeDtypeStruct((parts, slots, total), BF16),
        scratch_shapes=[pltpu.VMEM((slots, n), BF16)],
        compiler_params=params(),
        cost_estimate=cost(2 * slots * n * total * parts, 2 * parts * total * (n + slots)),
        name=name,
    )(adapter, *values)


def collect(adapter, moved, widths, name):
    n = adapter.shape[0]
    parts, slots, total = moved.shape

    def kernel(a_ref, m_ref, *refs):
        outs, p_ref = refs[:-1], refs[-1]

        @pl.when(pl.program_id(0) == 0)
        def _():
            p_ref[...] = placing_columns(a_ref[...], slots)

        at = 0
        for o_ref, width in zip(outs, widths):
            o_ref[...] = jnp.dot(
                p_ref[...], m_ref[0, :, at : at + width], preferred_element_type=F32
            ).astype(BF16)
            at += width

    return pl.pallas_call(
        kernel,
        grid=(parts,),
        in_specs=[
            pl.BlockSpec((n, 1), lambda j: (0, 0)),
            pl.BlockSpec((1, slots, total), lambda j: (j, 0, 0)),
        ],
        out_specs=[pl.BlockSpec((n, width), lambda j: (0, j)) for width in widths],
        out_shape=[jax.ShapeDtypeStruct((n, width * parts), BF16) for width in widths],
        scratch_shapes=[pltpu.VMEM((n, slots), BF16)],
        compiler_params=params(),
        cost_estimate=cost(2 * slots * n * total * parts, 2 * parts * total * (n + slots)),
        name=name,
    )(adapter, moved)


def take_weights(w_ref, pick_ref, t):
    rank = w_ref.shape[1]
    width = w_ref.shape[2]
    pick_ref[: PER * rank, :] = w_ref[pl.ds(PER * t, PER)].reshape(PER * rank, width)
    pick_ref[PER * rank :, :] = w_ref[GROUP - 1]


def by_tile(kernel, ins, out, scratch, flops, name):
    def spec(shape):
        if shape[1] == SLOTS:
            return pl.BlockSpec((shape[0], TILE, shape[2]), lambda t: (0, t, 0))
        return pl.BlockSpec(shape, lambda t: (0, 0, 0))

    moved = sum(v.size * v.dtype.itemsize for v in ins) + out.size * out.dtype.itemsize
    return pl.pallas_call(
        kernel,
        grid=(TILES,),
        in_specs=[spec(v.shape) for v in ins],
        out_specs=spec(out.shape),
        out_shape=out,
        scratch_shapes=scratch,
        compiler_params=params(),
        cost_estimate=cost(flops, moved),
        name=name,
    )(*ins)


def lowered_part(rows, shrink):
    sources, _, width = rows.shape
    count, rank = sources * TILE, shrink.shape[1]

    def kernel(x_ref, w_ref, o_ref, pick_ref):
        take_weights(w_ref, pick_ref, pl.program_id(0))
        dense = lax.dot_general(
            x_ref[...].reshape(count, width),
            pick_ref[...],
            (((1,), (1,)), ((), ())),
            preferred_element_type=F32,
        )
        block = row_block(count)
        total = jnp.zeros((count, rank), F32)
        for b in range(PER + 1):
            total = total + jnp.where(block == b, dense[:, b * rank : (b + 1) * rank], 0.0)
        o_ref[...] = total.reshape(sources, TILE, rank)

    return by_tile(
        kernel,
        (rows, shrink),
        jax.ShapeDtypeStruct((sources, SLOTS, rank), F32),
        [pltpu.VMEM(((PER + 1) * rank, width), BF16)],
        2 * TILES * count * (PER + 1) * rank * width,
        "lowered_part",
    )


def backward_part(rows, expand, split):
    sources, _, width = rows.shape
    count, rank = sources * TILE, expand.shape[1]

    def kernel(x_ref, w_ref, o_ref, pick_ref):
        take_weights(w_ref, pick_ref, pl.program_id(0))
        x = x_ref[...].reshape(count, width)

        def part(lo, hi):
            dense = lax.dot_general(
                x[:, lo:hi], pick_ref[:, lo:hi], (((1,), (1,)), ((), ())), preferred_element_type=F32
            )
            total = jnp.zeros((count, 2 * rank), F32)
            for p in range((PER + 1) // 2):
                piece = dense[:, 2 * rank * p : 2 * rank * (p + 1)]
                total = total + jnp.where(pair_mask(count, p), piece, 0.0)
            return total + pltpu.roll(total, rank, 1)

        first = iota((count, 2 * rank), 1) < rank
        both = jnp.where(first, part(0, split), part(split, width))
        o_ref[...] = both.reshape(sources, TILE, 2 * rank)

    return by_tile(
        kernel,
        (rows, expand),
        jax.ShapeDtypeStruct((sources, SLOTS, 2 * rank), F32),
        [pltpu.VMEM(((PER + 1) * rank, width), BF16)],
        2 * TILES * count * (PER + 1) * rank * width,
        "backward_part",
    )


def spread_pairs(values, count, rank):
    held = values.reshape(count, 2 * rank).astype(F32)
    turned = pltpu.roll(held, rank, 1)
    first = iota((count, 2 * rank), 1) < rank
    halves = (jnp.where(first, held, turned), jnp.where(first, turned, held))
    return [
        jnp.concatenate(
            [jnp.where(pair_mask(count, p), half, 0.0) for p in range((PER + 1) // 2)], axis=1
        ).astype(BF16)
        for half in halves
    ]


def spread_blocks(values, count, rank):
    held = values.reshape(count, rank).astype(F32)
    block = row_block(count)
    return jnp.concatenate(
        [jnp.where(block == b, held, 0.0) for b in range(PER + 1)], axis=1
    ).astype(BF16)


def expand_rows(lowered, expand, split):
    sources = lowered.shape[0]
    count, rank, width = sources * TILE, expand.shape[1], expand.shape[2]

    def kernel(l_ref, w_ref, o_ref, pick_ref):
        take_weights(w_ref, pick_ref, pl.program_id(0))
        halves = spread_pairs(l_ref[...], count, rank)
        for half, lo, hi in zip(halves, (0, split), (split, width)):
            result = SCALE * jnp.dot(half, pick_ref[:, lo:hi], preferred_element_type=F32)
            o_ref[:, :, lo:hi] = result.astype(BF16).reshape(sources, TILE, hi - lo)

    return by_tile(
        kernel,
        (lowered, expand),
        jax.ShapeDtypeStruct((sources, SLOTS, width), BF16),
        [pltpu.VMEM(((PER + 1) * rank, width), BF16)],
        2 * TILES * count * (PER + 1) * rank * width,
        "expand_rows",
    )


def token_rows(backward, shrink):
    sources = backward.shape[0]
    count, rank, width = sources * TILE, shrink.shape[1], shrink.shape[2]

    def kernel(b_ref, w_ref, o_ref, pick_ref):
        take_weights(w_ref, pick_ref, pl.program_id(0))
        wide = spread_blocks(b_ref[...], count, rank)
        result = jnp.dot(wide, pick_ref[...], preferred_element_type=F32)
        o_ref[...] = result.astype(BF16).reshape(sources, TILE, width)

    return by_tile(
        kernel,
        (backward, shrink),
        jax.ShapeDtypeStruct((sources, SLOTS, width), BF16),
        [pltpu.VMEM(((PER + 1) * rank, width), BF16)],
        2 * TILES * count * (PER + 1) * rank * width,
        "token_rows",
    )


def put_gradient(o_ref, last_ref, pieces, rank, lo, hi):
    t = pl.program_id(0)
    o_ref[pl.ds(PER * t, PER), :, lo:hi] = (
        pieces[: PER * rank].astype(BF16).reshape(PER, rank, hi - lo)
    )
    last = pieces[PER * rank :]

    @pl.when(t == 0)
    def _():
        last_ref[:, lo:hi] = last

    @pl.when(t > 0)
    def _():
        last_ref[:, lo:hi] = last_ref[:, lo:hi] + last

    @pl.when(t == TILES - 1)
    def _():
        o_ref[GROUP - 1, :, lo:hi] = last_ref[:, lo:hi].astype(BF16)


def expand_gradient(lowered, rows, rank, split):
    sources, _, width = rows.shape
    count = sources * TILE

    def kernel(l_ref, x_ref, o_ref, last_ref):
        x = x_ref[...].reshape(count, width)
        halves = spread_pairs(l_ref[...], count, rank)
        for half, lo, hi in zip(halves, (0, split), (split, width)):
            pieces = SCALE * lax.dot_general(
                half, x[:, lo:hi], (((0,), (0,)), ((), ())), preferred_element_type=F32
            )
            put_gradient(o_ref, last_ref, pieces, rank, lo, hi)

    return by_tile(
        kernel,
        (lowered, rows),
        jax.ShapeDtypeStruct((GROUP, rank, width), BF16),
        [pltpu.VMEM((rank, width), F32)],
        2 * TILES * count * (PER + 1) * rank * width,
        "expand_gradient",
    )


def shrink_gradient(backward, rows):
    sources, _, width = rows.shape
    count, rank = sources * TILE, backward.shape[2]

    def kernel(b_ref, x_ref, o_ref, last_ref):
        wide = spread_blocks(b_ref[...], count, rank)
        pieces = lax.dot_general(
            wide,
            x_ref[...].reshape(count, width),
            (((0,), (0,)), ((), ())),
            preferred_element_type=F32,
        )
        put_gradient(o_ref, last_ref, pieces, rank, 0, width)

    return by_tile(
        kernel,
        (backward, rows),
        jax.ShapeDtypeStruct((GROUP, rank, width), BF16),
        [pltpu.VMEM((rank, width), F32)],
        2 * TILES * count * (PER + 1) * rank * width,
        "shrink_gradient",
    )


ROUTE = ("y", "c", "x")
PARTS = ("y", "c")


def exchange(values, axes):
    return lax.all_to_all(values, axes, 0, 0, tiled=True)


def combine(partial, factor, parts):
    sources, slots, rank = partial.shape
    pieces = exchange(partial.reshape(parts, sources * slots // parts, rank), PARTS)
    total = (factor * jnp.sum(pieces.reshape(parts, -1, rank), axis=0)).astype(BF16)
    return lax.all_gather(total, PARTS, axis=0, tiled=True).reshape(sources, slots, rank)


def body(tokens, adapter_index, query_cotangent, value_cotangent, shrink, query_expand, value_expand):
    parts = lax.axis_size(PARTS)
    sources = lax.axis_size(ROUTE)
    groups = sources // parts
    slots = groups * SLOTS
    local, kinds, rank, width = shrink.shape
    value_width = value_expand.shape[2]
    both = width + value_width

    whole_shrink = lax.all_gather(shrink.reshape(local, kinds * rank, width), "z", axis=0, tiled=True)
    whole_expand = lax.all_gather(
        jnp.concatenate([query_expand, value_expand], axis=2), "z", axis=0, tiled=True
    )

    sent_tokens = place(adapter_index, (tokens,), parts, slots, "place_tokens")
    rows_tokens = exchange(sent_tokens.reshape(sources, SLOTS, width), ROUTE)
    sent_both = place(adapter_index, (query_cotangent, value_cotangent), parts, slots, "place_cotangents")
    rows_both = exchange(sent_both.reshape(sources, SLOTS, both), ROUTE)

    lowered = combine(lowered_part(rows_tokens, whole_shrink), 1.0, parts)
    out_both = exchange(expand_rows(lowered, whole_expand, width), ROUTE)
    backward = combine(backward_part(rows_both, whole_expand, width), SCALE, parts)
    out_tokens = exchange(token_rows(backward, whole_shrink), ROUTE)

    grad_expand = lax.psum_scatter(
        expand_gradient(lowered, rows_both, rank, width), "z", scatter_dimension=0, tiled=True
    ).astype(F32)
    grad_shrink = lax.psum_scatter(
        shrink_gradient(backward, rows_tokens), "z", scatter_dimension=0, tiled=True
    ).astype(F32)

    query_delta, value_delta = collect(
        adapter_index, out_both.reshape(parts, slots, both), (width, value_width), "collect_deltas"
    )
    (token_gradient,) = collect(
        adapter_index, out_tokens.reshape(parts, slots, width), (width,), "collect_tokens"
    )
    return (
        query_delta,
        value_delta,
        token_gradient,
        grad_shrink.reshape(local, kinds, rank, width),
        grad_expand[:, :, :width],
        grad_expand[:, :, width:],
    )


def solution(mesh):
    grid = Mesh(mesh.devices.reshape(4, 2, 4, 8), ("y", "c", "x", "z"))
    rows = P(("y", "c", "x", "z"), None)
    return jax.shard_map(
        body,
        mesh=grid,
        in_specs=(
            rows,
            rows,
            rows,
            rows,
            P(("x", "z"), None, None, PARTS),
            P(("x", "z"), None, PARTS),
            P(("x", "z"), None, PARTS),
        ),
        out_specs=(
            rows,
            rows,
            rows,
            P(("x", "z"), None, None, PARTS),
            P(("x", "z"), None, PARTS),
            P(("x", "z"), None, PARTS),
        ),
        check_vma=False,
    )
```

profile of v0, /device:TPU:7, one launch (start us, length us, event | category | flops | bytes accessed | tf_op | source)
XLA Modules:
  0.0 321.7 jit_solution(15771227241520247901)
XLA Ops:
  7.9 1.4 copy.18.a_ref
  9.3 6.8 %place_tokens.1 = bf16[8,192,1024]{2,1,0:T(8,128)(2,1)} custom-call(s32[128,1]{1,0:T(8,128)} %copy.18.a_ref, bf16[128,8192]{1,0:T(8,128)(2,1)} %refs_0_.2), custom_call_target="tpu_custom_call" | custom-call | flops 402653184 | bytes 5242880 | tf_op jit(solution)/shard_map/place_tokens/pallas_call | solution.py:94
  16.1 45.7 %all_to_all.30.x_ref = bf16[32,48,1024]{2,1,0:T(8,128)(2,1)} all-to-all(bf16[32,48,1024]{2,1,0:T(8,128)(2,1)} %bitcast.14), channel_id=1, replica_groups=mesh['y'=4,'c'=2,'x'=4,'z'=8] {'y','c','x'}, dimensions={0} | all-to-all | bytes 6291456 | tf_op jit(solution)/shard_map/all_to_all | solution.py:363
  61.8 5.5 %all-gather.3.cloned.1.call-done.w_ref = bf16[16,128,1024]{2,1,0:T(8,128)(2,1)} async-done(((bf16[2,128,1024]{2,1,0:T(8,128)(2,1)}), bf16[16,128,1024]{2,1,0:T(8,128)(2,1)}) %all-gather.3.cloned.1.call-update) | async-done | bytes 4194320 | tf_op jit(solution)/shard_map/all_gather | solution.py:382
  67.3 6.6 %lowered_part.1 = f32[32,48,128]{2,1,0:T(8,128)} custom-call(bf16[32,48,1024]{2,1,0:T(8,128)(2,1)} %all_to_all.30.x_ref, bf16[16,128,1024]{2,1,0:T(8,128)(2,1)} %all-gather.3.cloned.1.call-done.w_ref), custom_call_target="tpu_custom_call" | custom-call | flops 2415919104 | bytes 8126464 | tf_op jit(solution)/shard_map/lowered_part/pallas_call | solution.py:156
  73.9 5.1 %all-to-all-start.1 = ((f32[8,192,128]{2,1,0:T(8,128)}), f32[8,192,128]{2,1,0:T(8,128)S(1)}, u32[]{:S(2)}, u32[]{:S(2)}) async-start(f32[8,192,128]{2,1,0:T(8,128)} %bitcast.18), calls=%async_computation.1 | async-start | bytes 1572864 | tf_op jit(solution)/shard_map/all_to_all | solution.py:363
  79.1 0.7 pad_maximum_fusion
  79.8 6.9 %place_cotangents.1 = bf16[8,192,1152]{2,1,0:T(8,128)(2,1)} custom-call(s32[128,1]{1,0:T(8,128)} %copy.18.a_ref, bf16[128,8192]{1,0:T(8,128)(2,1)} %refs_0_.3, bf16[128,1024]{1,0:T(8,128)(2,1)} %refs_1_.1), custom_call_target="tpu_custom_call" | custom-call | flops 452984832 | bytes 5898240 | tf_op jit(solution)/shard_map/place_cotangents/pallas_call | solution.py:94
  86.8 4.5 %all-to-all-done.1 = f32[8,192,128]{2,1,0:T(8,128)S(1)} async-done(((f32[8,192,128]{2,1,0:T(8,128)}), f32[8,192,128]{2,1,0:T(8,128)S(1)}, u32[]{:S(2)}, u32[]{:S(2)}) %all-to-all-start.1) | async-done | bytes 786464 | tf_op jit(solution)/shard_map/all_to_all | solution.py:363
  91.2 0.9 copy-done.3
  92.1 6.1 %all-to-all-start.3 = ((bf16[32,48,1152]{2,1,0:T(8,128)(2,1)}), bf16[32,48,1152]{2,1,0:T(8,128)(2,1)S(1)}, u32[]{:S(2)}, u32[]{:S(2)}) async-start(bf16[32,48,1152]{2,1,0:T(8,128)(2,1)} %bitcast.12), calls=%async_computation.3 | async-start | bytes 7077888 | tf_op jit(solution)/shard_map/all_to_all | solution.py:363
  98.3 1.8 reduce_sum.18
  100.1 47.8 %all_gather.13 = bf16[1536,128]{1,0:T(8,128)(2,1)} all-gather(bf16[192,128]{1,0:T(8,128)(2,1)} %reduce_sum.18), channel_id=1, replica_groups=mesh['y'=4,'c'=2,'x'=4,'z'=8] {'y','c'}, dimensions={0}, use_global_device_ids=true | all-gather | bytes 442368 | tf_op jit(solution)/shard_map/all_gather | solution.py:370
  147.9 1.8 copy-done
  149.7 6.7 %expand_gradient.1 = bf16[16,64,1152]{2,1,0:T(8,128)(2,1)} custom-call(bf16[32,48,128]{2,1,0:T(8,128)(2,1)} %bitcast.15, bf16[32,48,1152]{2,1,0:T(8,128)(2,1)} %copy-done), custom_call_target="tpu_custom_call" | custom-call | flops 1358954496 | bytes 6291456 | tf_op jit(solution)/shard_map/expand_gradient/pallas_call | solution.py:156
  156.4 6.1 %backward_part.1 = f32[32,48,128]{2,1,0:T(8,128)} custom-call(bf16[32,48,1152]{2,1,0:T(8,128)(2,1)} %copy-done, bf16[16,64,1152]{2,1,0:T(8,128)(2,1)} %all-gather.5.cloned.1.call-done.w_ref), custom_call_target="tpu_custom_call" | custom-call | flops 1358954496 | bytes 6684672 | tf_op jit(solution)/shard_map/backward_part/pallas_call | solution.py:156
  162.5 15.7 %all_to_all.31 = f32[8,192,128]{2,1,0:T(8,128)S(1)} all-to-all(f32[8,192,128]{2,1,0:T(8,128)} %bitcast.17), channel_id=1, replica_groups=mesh['y'=4,'c'=2,'x'=4,'z'=8] {'y','c'}, dimensions={0} | all-to-all | bytes 1572864 | tf_op jit(solution)/shard_map/all_to_all | solution.py:363
  178.3 14.9 %all_gather.15 = bf16[1536,128]{1,0:T(8,128)(2,1)} all-gather(bf16[192,128]{1,0:T(8,128)(2,1)S(1)} %multiply_convert_fusion), channel_id=1, replica_groups=mesh['y'=4,'c'=2,'x'=4,'z'=8] {'y','c'}, dimensions={0}, use_global_device_ids=true | all-gather | bytes 442368 | tf_op jit(solution)/shard_map/all_gather | solution.py:370
  193.2 6.8 %shrink_gradient.1 = bf16[16,128,1024]{2,1,0:T(8,128)(2,1)} custom-call(bf16[32,48,128]{2,1,0:T(8,128)(2,1)} %bitcast.21, bf16[32,48,1024]{2,1,0:T(8,128)(2,1)} %all_to_all.30.x_ref), custom_call_target="tpu_custom_call" | custom-call | flops 2415919104 | bytes 7733248 | tf_op jit(solution)/shard_map/shrink_gradient/pallas_call | solution.py:156
  200.1 6.3 %token_rows.1 = bf16[32,48,1024]{2,1,0:T(8,128)(2,1)} custom-call(bf16[32,48,128]{2,1,0:T(8,128)(2,1)} %bitcast.22, bf16[16,128,1024]{2,1,0:T(8,128)(2,1)} %all-gather.3.cloned.1.call-done.w_ref), custom_call_target="tpu_custom_call" | custom-call | flops 2415919104 | bytes 7733248 | tf_op jit(solution)/shard_map/token_rows/pallas_call | solution.py:156
  206.4 5.9 %all-to-all-start.5 = ((bf16[32,48,1024]{2,1,0:T(8,128)(2,1)}), bf16[32,48,1024]{2,1,0:T(8,128)(2,1)S(1)}, u32[]{:S(2)}, u32[]{:S(2)}) async-start(bf16[32,48,1024]{2,1,0:T(8,128)(2,1)} %token_rows.1), calls=%async_computation.5 | async-start | bytes 6291456 | tf_op jit(solution)/shard_map/all_to_all | solution.py:363
  212.3 5.7 %expand_rows.1 = bf16[32,48,1152]{2,1,0:T(8,128)(2,1)} custom-call(bf16[32,48,128]{2,1,0:T(8,128)(2,1)} %bitcast.16, bf16[16,64,1152]{2,1,0:T(8,128)(2,1)} %all-gather.5.cloned.1.call-done.w_ref), custom_call_target="tpu_custom_call" | custom-call | flops 1358954496 | bytes 6291456 | tf_op jit(solution)/shard_map/expand_rows/pallas_call | solution.py:156
  218.0 33.0 %all-to-all-done.5 = bf16[32,48,1024]{2,1,0:T(8,128)(2,1)S(1)} async-done(((bf16[32,48,1024]{2,1,0:T(8,128)(2,1)}), bf16[32,48,1024]{2,1,0:T(8,128)(2,1)S(1)}, u32[]{:S(2)}, u32[]{:S(2)}) %all-to-all-start.5) | async-done | bytes 3145760 | tf_op jit(solution)/shard_map/all_to_all | solution.py:363
  251.0 1.7 copy-done.2
  252.7 5.1 %all-to-all-start.2 = ((bf16[32,48,1152]{2,1,0:T(8,128)(2,1)}), bf16[32,48,1152]{2,1,0:T(8,128)(2,1)S(1)}, u32[]{:S(2)}, u32[]{:S(2)}) async-start(bf16[32,48,1152]{2,1,0:T(8,128)(2,1)} %expand_rows.1), calls=%async_computation.2 | async-start | bytes 7077888 | tf_op jit(solution)/shard_map/all_to_all | solution.py:363
  257.8 6.9 %collect_tokens.1 = bf16[128,8192]{1,0:T(8,128)(2,1)} custom-call(s32[128,1]{1,0:T(8,128)} %copy.18.a_ref, bf16[8,192,1024]{2,1,0:T(8,128)(2,1)} %bitcast.13), custom_call_target="tpu_custom_call" | custom-call | flops 402653184 | bytes 5242880 | tf_op jit(solution)/shard_map/collect_tokens/pallas_call | solution.py:126
  264.7 36.4 %all-to-all-done.2 = bf16[32,48,1152]{2,1,0:T(8,128)(2,1)S(1)} async-done(((bf16[32,48,1152]{2,1,0:T(8,128)(2,1)}), bf16[32,48,1152]{2,1,0:T(8,128)(2,1)S(1)}, u32[]{:S(2)}, u32[]{:S(2)}) %all-to-all-start.2) | async-done | bytes 3538976 | tf_op jit(solution)/shard_map/all_to_all | solution.py:363
  301.1 1.7 copy-done.1
  302.8 7.0 %collect_deltas.1 = (bf16[128,8192]{1,0:T(8,128)(2,1)}, bf16[128,1024]{1,0:T(8,128)(2,1)}) custom-call(s32[128,1]{1,0:T(8,128)} %copy.18.a_ref, bf16[8,192,1152]{2,1,0:T(8,128)(2,1)} %bitcast.11), custom_call_target="tpu_custom_call" | custom-call | flops 452984832 | bytes 5898240 | tf_op jit(solution)/shard_map/collect_deltas/pallas_call | solution.py:126
  309.8 1.4 slice.9
  311.2 1.8 slice.8
  313.0 2.1 convert.1
  (22 shorter events, 0.9 us)
Async XLA Ops:
  7.2 60.1 %all-gather.3.cloned.1.call-start = ((), (), s32[]{:S(2)}) async-start(), calls=%async_computation.8 | async-start | bytes 4718592 | tf_op jit(solution)/shard_map/all_gather | solution.py:382
  61.8 17.3 %copy-start.4 = (bf16[2,64,1024]{2,1,0:T(8,128)(2,1)S(1)}, bf16[2,64,1024]{2,1,0:T(8,128)(2,1)}, u32[]{:S(2)}) copy-start(bf16[2,64,1024]{2,1,0:T(8,128)(2,1)} %param.12) | copy-start | bytes 786436
  61.8 17.3 %copy-start.5 = (bf16[2,64,128]{2,1,0:T(8,128)(2,1)S(1)}, bf16[2,64,128]{2,1,0:T(8,128)(2,1)}, u32[]{:S(2)}) copy-start(bf16[2,64,128]{2,1,0:T(8,128)(2,1)} %param.13) | copy-start | bytes 98308
  73.9 17.3 %all-to-all-start.1 = ((f32[8,192,128]{2,1,0:T(8,128)}), f32[8,192,128]{2,1,0:T(8,128)S(1)}, u32[]{:S(2)}, u32[]{:S(2)}) async-start(f32[8,192,128]{2,1,0:T(8,128)} %bitcast.18), calls=%async_computation.1 | async-start | bytes 1572864 | tf_op jit(solution)/shard_map/all_to_all | solution.py:363
  79.1 77.4 %all-gather.5.cloned.1.call-start = ((), (), s32[]{:S(2)}) async-start(), calls=%async_computation.9 | async-start | bytes 2654208 | tf_op jit(solution)/shard_map/all_gather | solution.py:383
  91.2 0.9 copy-start.3
  92.1 55.8 %all-to-all-start.3 = ((bf16[32,48,1152]{2,1,0:T(8,128)(2,1)}), bf16[32,48,1152]{2,1,0:T(8,128)(2,1)S(1)}, u32[]{:S(2)}, u32[]{:S(2)}) async-start(bf16[32,48,1152]{2,1,0:T(8,128)(2,1)} %bitcast.12), calls=%async_computation.3 | async-start | bytes 7077888 | tf_op jit(solution)/shard_map/all_to_all | solution.py:363
  98.2 211.6 %reduce-scatter.5.cloned.1.call-start = ((), (), s32[]{:S(2)}) async-start(), calls=%async_computation.11 | async-start | bytes 2654208 | tf_op jit(solution)/shard_map/reduce_scatter | solution.py:397
  147.9 1.8 copy-start
  156.3 156.7 %reduce-scatter.3.cloned.1.call-start = ((), (), s32[]{:S(2)}) async-start(), calls=%async_computation.10 | async-start | bytes 4718592 | tf_op jit(solution)/shard_map/reduce_scatter | solution.py:400
  206.4 44.6 %all-to-all-start.5 = ((bf16[32,48,1024]{2,1,0:T(8,128)(2,1)}), bf16[32,48,1024]{2,1,0:T(8,128)(2,1)S(1)}, u32[]{:S(2)}, u32[]{:S(2)}) async-start(bf16[32,48,1024]{2,1,0:T(8,128)(2,1)} %token_rows.1), calls=%async_computation.5 | async-start | bytes 6291456 | tf_op jit(solution)/shard_map/all_to_all | solution.py:363
  251.0 1.7 copy-start.2
  252.7 48.4 %all-to-all-start.2 = ((bf16[32,48,1152]{2,1,0:T(8,128)(2,1)}), bf16[32,48,1152]{2,1,0:T(8,128)(2,1)S(1)}, u32[]{:S(2)}, u32[]{:S(2)}) async-start(bf16[32,48,1152]{2,1,0:T(8,128)(2,1)} %expand_rows.1), calls=%async_computation.2 | async-start | bytes 7077888 | tf_op jit(solution)/shard_map/all_to_all | solution.py:363
  301.1 1.7 copy-start.1
Sparse Core Ops, SparseCore 0:
  9.8 57.4 all-gather.2
  82.2 35.9 all-gather.4
  156.5 36.8 reduce-scatter.4
  200.2 53.8 reduce-scatter.2
where the time goes:
time: 323 us; the launch traced here: 322 us
  blocking collectives  124 us (38%)
  waiting for transfers between devices  80.1 us (25%)
  Pallas kernels  65.8 us (20%)
  starting transfers between devices  22.4 us (7%)
  between operations  13.8 us (4%)
  local copies, waits for them, and re-layouts  10.7 us (3%)
  other arithmetic  4.74 us (1%)
    all_to_all x4, waiting for transfers between devices, exchange(): return lax.all_to_all(values, axes, 0, 0, tiled=True)  73.8 us
    all_gather x2, blocking collectives, combine(): lax.all_gather(total, PARTS, axis=0, tiled=True)  62.7 us
    all_to_all x2, blocking collectives, exchange(): return lax.all_to_all(values, axes, 0, 0, tiled=True)  61.4 us
    pallas_call x6, Pallas kernels, by_tile(): pl.pallas_call(kernel, grid=(TILES,), in_specs=[spec(v.shape) for v in in...  38.2 us
    all_to_all x4, starting transfers between devices, exchange(): return lax.all_to_all(values, axes, 0, 0, tiled=True)  22.3 us
    pallas_call x2, Pallas kernels, collect(): pl.pallas_call(kernel, grid=(parts,), in_specs=[pl.BlockSpec((n, 1), lamb...  13.9 us
    pallas_call x2, Pallas kernels, place(): pl.pallas_call(kernel, grid=(parts,), in_specs=[pl.BlockSpec((n, 1), lamb...  13.7 us
    unnamed x13, local copies, waits for them, and re-layouts  7.5 us
  transfers between devices with their start and end apart: 8, of which 4 were waited for; matrix products, arithmetic and copies ran while one was open for 2% of the time, Pallas kernels for 18%

commit v1 on v0

v1 whole, which is shorter than its diff:
```python
import jax
import jax.numpy as jnp
from jax import lax
from jax.experimental import pallas as pl
from jax.experimental.pallas import tpu as pltpu
from jax.sharding import Mesh, PartitionSpec as P


SCALE = 0.5
F32 = jnp.float32
BF16 = jnp.bfloat16
CAP = 3
PAIR = 2
CUTS = 8
BLOCKS = CUTS * PAIR
SLOTS = BLOCKS * CAP
TILE = 16
TILES = SLOTS // TILE
STEP = 5
HELD = STEP + 1
NEAR = 4


def iota(shape, dim):
    return lax.broadcasted_iota(jnp.int32, shape, dim)


def target_of(adapter, ordinal):
    dest = ((adapter >> 1) & 7) * 4 + (adapter >> 4)
    return dest * SLOTS + (adapter & 1) * CAP + ordinal


def as_row(column):
    n = column.shape[0]
    return jnp.sum(jnp.where(iota((n, n), 0) == iota((n, n), 1), column, 0), axis=0, keepdims=True)


def target_row(adapter):
    n = adapter.shape[0]
    row = as_row(adapter)
    same = (adapter == row) & (iota((n, n), 0) < iota((n, n), 1))
    return target_of(row, jnp.sum(same.astype(jnp.int32), axis=0, keepdims=True))


def target_column(adapter):
    n = adapter.shape[0]
    same = (adapter == as_row(adapter)) & (iota((n, n), 1) < iota((n, n), 0))
    return target_of(adapter, jnp.sum(same.astype(jnp.int32), axis=1, keepdims=True))


def slot_at(index, t):
    return (index >> 4) * SLOTS + t * TILE + (index & (TILE - 1))


def row_block(rows, t):
    inner = (iota((rows, 128), 0) & (TILE - 1)) + t
    block = jnp.zeros((rows, 128), jnp.int32)
    for k in range(1, HELD):
        block = block + (inner >= CAP * k).astype(jnp.int32)
    return block


def pair_of(block, pair):
    half = (iota(block.shape, 1) >= 64).astype(jnp.int32)
    return block == 2 * pair + half


def params():
    return pltpu.CompilerParams(vmem_limit_bytes=30 << 20)


def cost(flops, moved):
    return pl.CostEstimate(flops=flops, bytes_accessed=moved, transcendentals=0)


def place(adapter, values, sources):
    n = adapter.shape[0]
    widths = [v.shape[1] // CUTS for v in values]
    total = sum(widths)
    count = sources * TILE

    def kernel(a_ref, *refs):
        ins, o_ref = refs[:-1], refs[-1]
        t = pl.program_id(0)
        first = target_row(a_ref[...])
        slot = slot_at(iota((count, n), 0), t)
        spots = jnp.concatenate(
            [slot == first + PAIR * CAP * (2 * t + near) for near in range(NEAR)], axis=1
        )
        spots = spots.astype(F32).astype(BF16)
        at = 0
        for v_ref, width in zip(ins, widths):
            begin = pl.multiple_of(2 * t * width, 128)
            held = v_ref[:, pl.ds(begin, NEAR * width)]
            held = jnp.concatenate(
                [held[:, near * width : (near + 1) * width] for near in range(NEAR)], axis=0
            )
            moved = jnp.dot(spots, held, preferred_element_type=F32).astype(BF16)
            o_ref[:, :, at : at + width] = moved.reshape(sources, TILE, width)
            at += width

    return pl.pallas_call(
        kernel,
        grid=(TILES,),
        in_specs=[pl.BlockSpec((n, 1), lambda t: (0, 0))]
        + [pl.BlockSpec(v.shape, lambda t: (0, 0)) for v in values],
        out_specs=pl.BlockSpec((sources, TILE, total), lambda t: (0, t, 0)),
        out_shape=jax.ShapeDtypeStruct((sources, SLOTS, total), BF16),
        compiler_params=params(),
        cost_estimate=cost(2 * sources * SLOTS * n * NEAR * total, 2 * total * (CUTS * n + sources * SLOTS)),
    )(adapter, *values)


def collect(adapter, moved, widths):
    n = adapter.shape[0]
    sources, _, total = moved.shape
    count = sources * TILE

    def kernel(a_ref, m_ref, *outs):
        t = pl.program_id(0)
        first = target_column(a_ref[...])
        slot = slot_at(iota((n, count), 1), t)
        spots = jnp.concatenate(
            [slot == first + PAIR * CAP * (2 * t + near) for near in range(NEAR)], axis=0
        )
        spots = spots.astype(F32).astype(BF16)
        at = 0
        for o_ref, width in zip(outs, widths):
            found = jnp.dot(
                spots, m_ref[:, :, at : at + width].reshape(count, width), preferred_element_type=F32
            )
            for near in range(NEAR):
                here = pl.ds(pl.multiple_of((2 * t + near) * width, 128), width)
                piece = found[near * n : (near + 1) * n]
                if near < 2:
                    piece = piece + jnp.where(t > 0, o_ref[:, here].astype(F32), 0.0)
                o_ref[:, here] = piece.astype(BF16)
            at += width

    return pl.pallas_call(
        kernel,
        grid=(TILES,),
        in_specs=[
            pl.BlockSpec((n, 1), lambda t: (0, 0)),
            pl.BlockSpec((sources, TILE, total), lambda t: (0, t, 0)),
        ],
        out_specs=[pl.BlockSpec((n, width * CUTS), lambda t: (0, 0)) for width in widths],
        out_shape=[jax.ShapeDtypeStruct((n, width * CUTS), BF16) for width in widths],
        compiler_params=params(),
        cost_estimate=cost(2 * sources * SLOTS * n * NEAR * total, 2 * total * (CUTS * n + sources * SLOTS)),
    )(adapter, moved)


def held_weights(w_ref, t):
    _, rank, width = w_ref.shape
    return w_ref[pl.ds(STEP * t, HELD)].reshape(HELD * rank, width)


def by_tile(kernel, ins, out, scratch, flops, whole_out=False):
    def spec(shape):
        if shape[1] == SLOTS:
            return pl.BlockSpec((shape[0], TILE, shape[2]), lambda t: (0, t, 0))
        return pl.BlockSpec(shape, lambda t: (0, 0, 0))

    moved = sum(v.size * v.dtype.itemsize for v in ins) + out.size * out.dtype.itemsize
    return pl.pallas_call(
        kernel,
        grid=(TILES,),
        in_specs=[spec(v.shape) for v in ins],
        out_specs=pl.BlockSpec(out.shape, lambda t: (0, 0, 0)) if whole_out else spec(out.shape),
        out_shape=out,
        scratch_shapes=scratch,
        compiler_params=params(),
        cost_estimate=cost(flops, moved),
    )(*ins)


def sum_slices(part_ref, o_ref, factor):
    half = SLOTS // 2
    total = part_ref[:, :half, :] + part_ref[:, half:, :]
    total = total + pltpu.roll(total, half // 2, 1)
    total = total + pltpu.roll(total, half // 4, 1)
    o_ref[...] = (factor * jnp.concatenate([total, total], axis=1)).astype(BF16)


def keep_part(part_ref, t, part):
    for tile in range(TILES):

        @pl.when(t == tile)
        def _(tile=tile):
            part_ref[:, tile * TILE : (tile + 1) * TILE, :] = part


def lowered_rows(rows, shrink):
    sources, _, width = rows.shape
    count, rank = sources * TILE, shrink.shape[1]

    def kernel(x_ref, w_ref, o_ref, part_ref):
        t = pl.program_id(0)
        dense = lax.dot_general(
            x_ref[...].reshape(count, width),
            held_weights(w_ref, t),
            (((1,), (1,)), ((), ())),
            preferred_element_type=F32,
        )
        block = row_block(count, t)
        total = jnp.zeros((count, rank), F32)
        for b in range(HELD):
            total = total + jnp.where(block == b, dense[:, b * rank : (b + 1) * rank], 0.0)
        keep_part(part_ref, t, total.reshape(sources, TILE, rank))

        @pl.when(t == TILES - 1)
        def _():
            sum_slices(part_ref, o_ref, 1.0)

    return by_tile(
        kernel,
        (rows, shrink),
        jax.ShapeDtypeStruct((sources, SLOTS, rank), BF16),
        [pltpu.VMEM((sources, SLOTS, rank), F32)],
        2 * TILES * count * HELD * rank * width,
        whole_out=True,
    )


def backward_rows(rows, expand, split):
    sources, _, width = rows.shape
    count, rank = sources * TILE, expand.shape[1]

    def kernel(x_ref, w_ref, o_ref, part_ref):
        t = pl.program_id(0)
        x = x_ref[...].reshape(count, width)
        w = held_weights(w_ref, t)
        block = row_block(count, t)

        def part(lo, hi):
            dense = lax.dot_general(
                x[:, lo:hi], w[:, lo:hi], (((1,), (1,)), ((), ())), preferred_element_type=F32
            )
            total = jnp.zeros((count, 2 * rank), F32)
            for p in range(HELD // 2):
                piece = dense[:, 2 * rank * p : 2 * rank * (p + 1)]
                total = total + jnp.where(pair_of(block, p), piece, 0.0)
            return total + pltpu.roll(total, rank, 1)

        first = iota((count, 2 * rank), 1) < rank
        both = jnp.where(first, part(0, split), part(split, width))
        keep_part(part_ref, t, both.reshape(sources, TILE, 2 * rank))

        @pl.when(t == TILES - 1)
        def _():
            sum_slices(part_ref, o_ref, SCALE)

    return by_tile(
        kernel,
        (rows, expand),
        jax.ShapeDtypeStruct((sources, SLOTS, 2 * rank), BF16),
        [pltpu.VMEM((sources, SLOTS, 2 * rank), F32)],
        2 * TILES * count * HELD * rank * width,
        whole_out=True,
    )


def spread_pairs(values, count, rank, t):
    held = values.reshape(count, 2 * rank).astype(F32)
    turned = pltpu.roll(held, rank, 1)
    first = iota((count, 2 * rank), 1) < rank
    halves = (jnp.where(first, held, turned), jnp.where(first, turned, held))
    block = row_block(count, t)
    return [
        jnp.concatenate(
            [jnp.where(pair_of(block, p), half, 0.0) for p in range(HELD // 2)], axis=1
        ).astype(BF16)
        for half in halves
    ]


def spread_blocks(values, count, rank, t):
    held = values.reshape(count, rank).astype(F32)
    block = row_block(count, t)
    return jnp.concatenate(
        [jnp.where(block == b, held, 0.0) for b in range(HELD)], axis=1
    ).astype(BF16)


def expand_rows(lowered, expand, split):
    sources = lowered.shape[0]
    count, rank, width = sources * TILE, expand.shape[1], expand.shape[2]

    def kernel(l_ref, w_ref, o_ref):
        t = pl.program_id(0)
        w = held_weights(w_ref, t)
        halves = spread_pairs(l_ref[...], count, rank, t)
        for half, lo, hi in zip(halves, (0, split), (split, width)):
            result = SCALE * jnp.dot(half, w[:, lo:hi], preferred_element_type=F32)
            o_ref[:, :, lo:hi] = result.astype(BF16).reshape(sources, TILE, hi - lo)

    return by_tile(
        kernel,
        (lowered, expand),
        jax.ShapeDtypeStruct((sources, SLOTS, width), BF16),
        [],
        2 * TILES * count * HELD * rank * width,
    )


def token_rows(backward, shrink):
    sources = backward.shape[0]
    count, rank, width = sources * TILE, shrink.shape[1], shrink.shape[2]

    def kernel(b_ref, w_ref, o_ref):
        t = pl.program_id(0)
        wide = spread_blocks(b_ref[...], count, rank, t)
        result = jnp.dot(wide, held_weights(w_ref, t), preferred_element_type=F32)
        o_ref[...] = result.astype(BF16).reshape(sources, TILE, width)

    return by_tile(
        kernel,
        (backward, shrink),
        jax.ShapeDtypeStruct((sources, SLOTS, width), BF16),
        [],
        2 * TILES * count * HELD * rank * width,
    )


def put_gradient(o_ref, carry_ref, pieces, rank, lo, hi):
    t = pl.program_id(0)
    first = pieces[:rank] + jnp.where(t > 0, carry_ref[:, lo:hi], 0.0)
    o_ref[STEP * t, :, lo:hi] = first.astype(BF16)
    inner = pieces[rank : STEP * rank].astype(BF16)
    o_ref[pl.ds(STEP * t + 1, STEP - 1), :, lo:hi] = inner.reshape(STEP - 1, rank, hi - lo)
    last = pieces[STEP * rank :]
    carry_ref[:, lo:hi] = last

    @pl.when(t == TILES - 1)
    def _():
        o_ref[BLOCKS - 1, :, lo:hi] = last.astype(BF16)


def expand_gradient(lowered, rows, rank, split):
    sources, _, width = rows.shape
    count = sources * TILE

    def kernel(l_ref, x_ref, o_ref, carry_ref):
        x = x_ref[...].reshape(count, width)
        halves = spread_pairs(l_ref[...], count, rank, pl.program_id(0))
        for half, lo, hi in zip(halves, (0, split), (split, width)):
            pieces = SCALE * lax.dot_general(
                half, x[:, lo:hi], (((0,), (0,)), ((), ())), preferred_element_type=F32
            )
            put_gradient(o_ref, carry_ref, pieces, rank, lo, hi)

    return by_tile(
        kernel,
        (lowered, rows),
        jax.ShapeDtypeStruct((BLOCKS, rank, width), BF16),
        [pltpu.VMEM((rank, width), F32)],
        2 * TILES * count * HELD * rank * width,
    )


def shrink_gradient(backward, rows):
    sources, _, width = rows.shape
    count, rank = sources * TILE, backward.shape[2]

    def kernel(b_ref, x_ref, o_ref, carry_ref):
        wide = spread_blocks(b_ref[...], count, rank, pl.program_id(0))
        pieces = lax.dot_general(
            wide,
            x_ref[...].reshape(count, width),
            (((0,), (0,)), ((), ())),
            preferred_element_type=F32,
        )
        put_gradient(o_ref, carry_ref, pieces, rank, 0, width)

    return by_tile(
        kernel,
        (backward, rows),
        jax.ShapeDtypeStruct((BLOCKS, rank, width), BF16),
        [pltpu.VMEM((rank, width), F32)],
        2 * TILES * count * HELD * rank * width,
    )


ROUTE = ("y", "c", "x")
PARTS = ("y", "c")
SWAP = ("y", "c", "z")


def exchange(values):
    return lax.all_to_all(values, ROUTE, 0, 0, tiled=True)


def swap(values):
    turns = [(j * CUTS + o, o * CUTS + j) for j in range(CUTS) for o in range(CUTS)]
    return lax.ppermute(values, SWAP, turns)


def gathered(shard):
    return lax.all_gather(swap(shard), "z", axis=0, tiled=True)


def summed(parts):
    return swap(lax.psum_scatter(parts, "z", scatter_dimension=0, tiled=True))


def body(tokens, adapter_index, query_cotangent, value_cotangent, shrink, query_expand, value_expand):
    sources = lax.axis_size(ROUTE)
    local, kinds, rank, width = shrink.shape
    value_width = value_expand.shape[2]

    sent_both = place(adapter_index, (query_cotangent, value_cotangent), sources)
    rows_both = exchange(sent_both)
    whole_expand = gathered(jnp.concatenate([query_expand, value_expand], axis=2))
    whole_shrink = gathered(shrink.reshape(local, kinds * rank, width))
    sent_tokens = place(adapter_index, (tokens,), sources)
    rows_tokens = exchange(sent_tokens)

    backward = backward_rows(rows_both, whole_expand, width)
    out_tokens = exchange(token_rows(backward, whole_shrink))
    grad_shrink = summed(shrink_gradient(backward, rows_tokens)).astype(F32)
    lowered = lowered_rows(rows_tokens, whole_shrink)
    out_both = exchange(expand_rows(lowered, whole_expand, width))
    grad_expand = summed(expand_gradient(lowered, rows_both, rank, width)).astype(F32)

    (token_gradient,) = collect(adapter_index, out_tokens, (width,))
    query_delta, value_delta = collect(adapter_index, out_both, (width, value_width))
    return (
        query_delta,
        value_delta,
        token_gradient,
        grad_shrink.reshape(local, kinds, rank, width),
        grad_expand[:, :, :width],
        grad_expand[:, :, width:],
    )


def solution(mesh):
    grid = Mesh(mesh.devices.reshape(4, 2, 4, 8), ("y", "c", "x", "z"))
    rows = P(("y", "c", "x", "z"), None)
    weights = (
        P(("x", "z"), None, None, PARTS),
        P(("x", "z"), None, PARTS),
        P(("x", "z"), None, PARTS),
    )

    return jax.shard_map(
        body,
        mesh=grid,
        in_specs=(rows, rows, rows, rows) + weights,
        out_specs=(rows, rows, rows) + weights,
        check_vma=False,
    )
```

time: 323 us -> 371 us (1.15)
  the two profiles are of different devices: /device:TPU:7 before, /device:TPU:8 now
where the time goes in v1:
time: 371 us; the launch traced here: 370 us
  waiting for transfers between devices  230 us (62%)
  starting transfers between devices  49.4 us (13%)
  Pallas kernels  40.6 us (11%)
  local copies, waits for them, and re-layouts  32.7 us (9%)
  between operations  14 us (4%)
    all_to_all x4, waiting for transfers between devices, exchange(): return lax.all_to_all(values, ROUTE, 0, 0, tiled=True)  88.1 us
    reduce_scatter x2, waiting for transfers between devices, summed(): return swap(lax.psum_scatter(parts, 'z', scatter_dimension=0, tiled=True))  79.5 us
    ppermute x4, waiting for transfers between devices, swap(): return lax.ppermute(values, SWAP, turns)  62 us
    all_to_all x4, starting transfers between devices, exchange(): return lax.all_to_all(values, ROUTE, 0, 0, tiled=True)  34.4 us
    unnamed x47, local copies, waits for them, and re-layouts  29.5 us
    pallas_call x6, Pallas kernels, by_tile(): pl.pallas_call(kernel, grid=(TILES,), in_specs=[spec(v.shape) for v in in...  24.2 us
    ppermute x4, starting transfers between devices, swap(): return lax.ppermute(values, SWAP, turns)  14.8 us
    pallas_call x2, Pallas kernels, collect(): pl.pallas_call(kernel, grid=(TILES,), in_specs=[pl.BlockSpec((n, 1), lamb...  10.8 us
  transfers between devices with their start and end apart: 12, of which 7 were waited for; matrix products, arithmetic and copies ran while one was open for 1% of the time, Pallas kernels for 11%

profile of v1, /device:TPU:8, one launch (start us, length us, event | category | flops | bytes accessed | tf_op | source)
XLA Modules:
  0.0 369.6 jit_solution(16082552720469052343)
XLA Ops:
  8.2 5.1 %collective-permute-start.1 = (bf16[2,64,1152]{2,1,0:T(8,128)(2,1)S(1)}, bf16[2,64,1152]{2,1,0:T(8,128)(2,1)S(1)}, u32[]{:S(2)}, u32[]{:S(2)}) collective-permute-start(bf16[2,64,1152]{2,1,0:T(8,128)(2,1)S(1)} %pad_maximum_fusion), channel_id=1, source_target_pairs={{0,0},{1,32},{2,64},{3,96},{4,128},{5,160},{6,192},{7,224},{32,1},... | collective-permute-start | bytes 884744 | tf_op jit(solution)/shard_map/ppermute | solution.py:396
  13.3 21.0 %collective-permute-done.1 = bf16[2,64,1152]{2,1,0:T(8,128)(2,1)S(1)} collective-permute-done((bf16[2,64,1152]{2,1,0:T(8,128)(2,1)S(1)}, bf16[2,64,1152]{2,1,0:T(8,128)(2,1)S(1)}, u32[]{:S(2)}, u32[]{:S(2)}) %collective-permute-start.1) | collective-permute-done | bytes 294944 | tf_op jit(solution)/shard_map/ppermute | solution.py:396
  35.1 1.9 collective-permute-start
  37.0 32.1 %collective-permute-done = bf16[2,128,1024]{2,1,0:T(8,128)(2,1)S(1)} collective-permute-done((bf16[2,128,1024]{2,1,0:T(8,128)(2,1)}, bf16[2,128,1024]{2,1,0:T(8,128)(2,1)S(1)}, u32[]{:S(2)}, u32[]{:S(2)}) %collective-permute-start) | collective-permute-done | bytes 524320 | tf_op jit(solution)/shard_map/ppermute | solution.py:396
  73.2 3.0 shard_map.122
  76.3 1.7 copy-done.4
  78.0 19.1 %all-to-all-start.2 = ((bf16[32,48,1152]{2,1,0:T(8,128)(2,1)}), bf16[32,48,1152]{2,1,0:T(8,128)(2,1)S(1)}, u32[]{:S(2)}, u32[]{:S(2)}) async-start(bf16[32,48,1152]{2,1,0:T(8,128)(2,1)} %copy-done.4), calls=%async_computation.2 | async-start | bytes 7077888 | tf_op jit(solution)/shard_map/all_to_all | solution.py:391
  99.6 2.6 shard_map.118
  103.8 36.3 %all-to-all-done.2.x_ref = bf16[32,48,1152]{2,1,0:T(8,128)(2,1)S(1)} async-done(((bf16[32,48,1152]{2,1,0:T(8,128)(2,1)}), bf16[32,48,1152]{2,1,0:T(8,128)(2,1)S(1)}, u32[]{:S(2)}, u32[]{:S(2)}) %all-to-all-start.2) | async-done | bytes 3538976 | tf_op jit(solution)/shard_map/all_to_all | solution.py:391
  140.1 5.5 %all-to-all-start = ((bf16[32,48,1024]{2,1,0:T(8,128)(2,1)}), bf16[32,48,1024]{2,1,0:T(8,128)(2,1)}, u32[]{:S(2)}, u32[]{:S(2)}) async-start(bf16[32,48,1024]{2,1,0:T(8,128)(2,1)} %copy-done.6), calls=%async_computation | async-start | bytes 6291456 | tf_op jit(solution)/shard_map/all_to_all | solution.py:391
  145.6 1.7 copy-done
  147.3 3.5 shard_map.123.b_ref
  151.6 32.8 %all-to-all-done.x_ref = bf16[32,48,1024]{2,1,0:T(8,128)(2,1)} async-done(((bf16[32,48,1024]{2,1,0:T(8,128)(2,1)}), bf16[32,48,1024]{2,1,0:T(8,128)(2,1)}, u32[]{:S(2)}, u32[]{:S(2)}) %all-to-all-start) | async-done | bytes 3145760 | tf_op jit(solution)/shard_map/all_to_all | solution.py:391
  185.4 4.7 %shard_map.126 = bf16[16,128,1024]{2,1,0:T(8,128)(2,1)S(1)} custom-call(bf16[32,48,128]{2,1,0:T(8,128)(2,1)S(1)} %copy-done.10, bf16[32,48,1024]{2,1,0:T(8,128)(2,1)} %all-to-all-done.x_ref), custom_call_target="tpu_custom_call" | custom-call | flops 2415919104 | bytes 7733248 | tf_op jit(solution)/shard_map/pallas_call | solution.py:166
  190.1 2.0 copy-done.3
  193.1 2.2 copy-done.16
  195.3 3.3 shard_map.124
  200.3 4.9 %all-to-all-start.3 = ((bf16[32,48,1024]{2,1,0:T(8,128)(2,1)}), bf16[32,48,1024]{2,1,0:T(8,128)(2,1)}, u32[]{:S(2)}, u32[]{:S(2)}) async-start(bf16[32,48,1024]{2,1,0:T(8,128)(2,1)} %copy-done.5), calls=%async_computation.3 | async-start | bytes 6291456 | tf_op jit(solution)/shard_map/all_to_all | solution.py:391
  205.3 2.2 copy-done.17
  207.5 4.8 %shard_map.119.l_ref = bf16[32,48,128]{2,1,0:T(8,128)(2,1)S(1)} custom-call(bf16[32,48,1024]{2,1,0:T(8,128)(2,1)} %all-to-all-done.x_ref, bf16[16,128,1024]{2,1,0:T(8,128)(2,1)S(1)} %copy-done.17), custom_call_target="tpu_custom_call" | custom-call | flops 2415919104 | bytes 7733248 | tf_op jit(solution)/shard_map/pallas_call | solution.py:166
  212.3 3.9 %shard_map.127 = bf16[16,64,1152]{2,1,0:T(8,128)(2,1)S(1)} custom-call(bf16[32,48,128]{2,1,0:T(8,128)(2,1)S(1)} %shard_map.119.l_ref, bf16[32,48,1152]{2,1,0:T(8,128)(2,1)S(1)} %all-to-all-done.2.x_ref), custom_call_target="tpu_custom_call" | custom-call | flops 1358954496 | bytes 6291456 | tf_op jit(solution)/shard_map/pallas_call | solution.py:166
  221.0 4.0 %shard_map.120 = bf16[32,48,1152]{2,1,0:T(8,128)(2,1)} custom-call(bf16[32,48,128]{2,1,0:T(8,128)(2,1)S(1)} %copy-done.8, bf16[16,64,1152]{2,1,0:T(8,128)(2,1)S(1)} %copy-done.1), custom_call_target="tpu_custom_call" | custom-call | flops 1358954496 | bytes 6291456 | tf_op jit(solution)/shard_map/pallas_call | solution.py:166
  225.0 19.0 %all-to-all-done.3.m_ref = bf16[32,48,1024]{2,1,0:T(8,128)(2,1)} async-done(((bf16[32,48,1024]{2,1,0:T(8,128)(2,1)}), bf16[32,48,1024]{2,1,0:T(8,128)(2,1)}, u32[]{:S(2)}, u32[]{:S(2)}) %all-to-all-start.3) | async-done | bytes 3145760 | tf_op jit(solution)/shard_map/all_to_all | solution.py:391
  244.0 4.9 %all-to-all-start.1 = ((bf16[32,48,1152]{2,1,0:T(8,128)(2,1)}), bf16[32,48,1152]{2,1,0:T(8,128)(2,1)S(1)}, u32[]{:S(2)}, u32[]{:S(2)}) async-start(bf16[32,48,1152]{2,1,0:T(8,128)(2,1)} %shard_map.120), calls=%async_computation.1 | async-start | bytes 7077888 | tf_op jit(solution)/shard_map/all_to_all | solution.py:391
  249.0 5.9 %collective-permute-start.2 = (bf16[2,128,1024]{2,1,0:T(8,128)(2,1)}, bf16[2,128,1024]{2,1,0:T(8,128)(2,1)}, u32[]{:S(2)}, u32[]{:S(2)}) collective-permute-start(bf16[2,128,1024]{2,1,0:T(8,128)(2,1)} %reduce-scatter.3.cloned.1.call-done), channel_id=1, source_target_pairs={{0,0},{1,32},{2,64},{3,96},{4,128},{5,160},{6,192},{7,224},{32,1},... | collective-permute-start | bytes 1572872 | tf_op jit(solution)/shard_map/ppermute | solution.py:396
  254.9 79.5 %reduce-scatter.5.cloned.1.call-done = bf16[2,64,1152]{2,1,0:T(8,128)(2,1)} async-done(((bf16[16,64,1152]{2,1,0:T(8,128)(2,1)}), bf16[2,64,1152]{2,1,0:T(8,128)(2,1)}) %reduce-scatter.5.cloned.1.call-update) | async-done | bytes 294928 | tf_op jit(solution)/shard_map/reduce_scatter | solution.py:404
  334.5 1.9 collective-permute-start.3
  337.2 5.7 %shard_map.125 = bf16[128,8192]{1,0:T(8,128)(2,1)} custom-call(s32[128,1]{1,0:T(8,128)S(1)} %copy-done.14, bf16[32,48,1024]{2,1,0:T(8,128)(2,1)} %all-to-all-done.3.m_ref), custom_call_target="tpu_custom_call" | custom-call | flops 1610612736 | bytes 5242880 | tf_op jit(solution)/shard_map/pallas_call | solution.py:140
  343.8 5.1 %shard_map.121 = (bf16[128,8192]{1,0:T(8,128)(2,1)}, bf16[128,1024]{1,0:T(8,128)(2,1)}) custom-call(s32[128,1]{1,0:T(8,128)S(1)} %copy-done.15, bf16[32,48,1152]{2,1,0:T(8,128)(2,1)S(1)} %all-to-all-done.1.m_ref), custom_call_target="tpu_custom_call" | custom-call | flops 1811939328 | bytes 5898240 | tf_op jit(solution)/shard_map/pallas_call | solution.py:140
  348.9 8.9 %collective-permute-done.3 = bf16[2,64,1152]{2,1,0:T(8,128)(2,1)} collective-permute-done((bf16[2,64,1152]{2,1,0:T(8,128)(2,1)}, bf16[2,64,1152]{2,1,0:T(8,128)(2,1)}, u32[]{:S(2)}, u32[]{:S(2)}) %collective-permute-start.3) | collective-permute-done | bytes 294944 | tf_op jit(solution)/shard_map/ppermute | solution.py:396
  359.2 1.8 slice.8
  361.0 2.1 convert.1
  (57 shorter events, 22.4 us)
Async XLA Ops:
  7.2 138.5 %all-gather.5.cloned.1.call-start = ((), (), s32[]{:S(2)}) async-start(), calls=%async_computation.7 | async-start | bytes 2654208 | tf_op jit(solution)/shard_map/all_gather | solution.py:400
  8.2 26.1 %collective-permute-start.1 = (bf16[2,64,1152]{2,1,0:T(8,128)(2,1)S(1)}, bf16[2,64,1152]{2,1,0:T(8,128)(2,1)S(1)}, u32[]{:S(2)}, u32[]{:S(2)}) collective-permute-start(bf16[2,64,1152]{2,1,0:T(8,128)(2,1)S(1)} %pad_maximum_fusion), channel_id=1, source_target_pairs={{0,0},{1,32},{2,64},{3,96},{4,128},{5,160},{6,192},{7,224},{32,1},... | collective-permute-start | bytes 884744 | tf_op jit(solution)/shard_map/ppermute | solution.py:396
  35.0 157.1 %all-gather.3.cloned.1.call-start = ((), (), s32[]{:S(2)}) async-start(), calls=%async_computation.6 | async-start | bytes 4718592 | tf_op jit(solution)/shard_map/all_gather | solution.py:400
  35.1 34.0 %collective-permute-start = (bf16[2,128,1024]{2,1,0:T(8,128)(2,1)}, bf16[2,128,1024]{2,1,0:T(8,128)(2,1)S(1)}, u32[]{:S(2)}, u32[]{:S(2)}) collective-permute-start(bf16[2,128,1024]{2,1,0:T(8,128)(2,1)} %bitcast.3), channel_id=1, source_target_pairs={{0,0},{1,32},{2,64},{3,96},{4,128},{5,160},{6,192},{7,224},{32,1},... | collective-permute-start | bytes 1572872 | tf_op jit(solution)/shard_map/ppermute | solution.py:396
  69.1 0.8 copy-start.21
  70.7 1.6 copy-start.18
  72.3 0.9 copy-start.20
  73.2 3.1 copy-start.12
  76.3 1.7 copy-start.4
  78.0 62.1 %all-to-all-start.2 = ((bf16[32,48,1152]{2,1,0:T(8,128)(2,1)}), bf16[32,48,1152]{2,1,0:T(8,128)(2,1)S(1)}, u32[]{:S(2)}, u32[]{:S(2)}) async-start(bf16[32,48,1152]{2,1,0:T(8,128)(2,1)} %copy-done.4), calls=%async_computation.2 | async-start | bytes 7077888 | tf_op jit(solution)/shard_map/all_to_all | solution.py:391
  97.1 0.8 copy-start.13
  98.0 1.6 copy-start.19
  102.2 1.6 copy-start.6
  140.1 44.3 %all-to-all-start = ((bf16[32,48,1024]{2,1,0:T(8,128)(2,1)}), bf16[32,48,1024]{2,1,0:T(8,128)(2,1)}, u32[]{:S(2)}, u32[]{:S(2)}) async-start(bf16[32,48,1024]{2,1,0:T(8,128)(2,1)} %copy-done.6), calls=%async_computation | async-start | bytes 6291456 | tf_op jit(solution)/shard_map/all_to_all | solution.py:391
  145.6 103.5 %reduce-scatter.3.cloned.1.call-start = ((), (), s32[]{:S(2)}) async-start(), calls=%async_computation.8 | async-start | bytes 4718592 | tf_op jit(solution)/shard_map/reduce_scatter | solution.py:404
  145.6 1.7 copy-start
  184.4 1.0 copy-start.10
  190.1 2.0 copy-start.3
  192.1 1.0 copy-start.11
  193.1 2.2 copy-start.16
  198.6 1.7 copy-start.5
  200.3 43.7 %all-to-all-start.3 = ((bf16[32,48,1024]{2,1,0:T(8,128)(2,1)}), bf16[32,48,1024]{2,1,0:T(8,128)(2,1)}, u32[]{:S(2)}, u32[]{:S(2)}) async-start(bf16[32,48,1024]{2,1,0:T(8,128)(2,1)} %copy-done.5), calls=%async_computation.3 | async-start | bytes 6291456 | tf_op jit(solution)/shard_map/all_to_all | solution.py:391
  205.2 129.2 %reduce-scatter.5.cloned.1.call-start = ((), (), s32[]{:S(2)}) async-start(), calls=%async_computation.9 | async-start | bytes 2654208 | tf_op jit(solution)/shard_map/reduce_scatter | solution.py:404
  205.3 2.2 copy-start.17
  216.2 1.4 copy-start.2
  218.3 1.7 copy-start.1
  220.0 1.0 copy-start.8
  244.0 98.9 %all-to-all-start.1 = ((bf16[32,48,1152]{2,1,0:T(8,128)(2,1)}), bf16[32,48,1152]{2,1,0:T(8,128)(2,1)S(1)}, u32[]{:S(2)}, u32[]{:S(2)}) async-start(bf16[32,48,1152]{2,1,0:T(8,128)(2,1)} %shard_map.120), calls=%async_computation.1 | async-start | bytes 7077888 | tf_op jit(solution)/shard_map/all_to_all | solution.py:391
  249.0 111.9 %collective-permute-start.2 = (bf16[2,128,1024]{2,1,0:T(8,128)(2,1)}, bf16[2,128,1024]{2,1,0:T(8,128)(2,1)}, u32[]{:S(2)}, u32[]{:S(2)}) collective-permute-start(bf16[2,128,1024]{2,1,0:T(8,128)(2,1)} %reduce-scatter.3.cloned.1.call-done), channel_id=1, source_target_pairs={{0,0},{1,32},{2,64},{3,96},{4,128},{5,160},{6,192},{7,224},{32,1},... | collective-permute-start | bytes 1572872 | tf_op jit(solution)/shard_map/ppermute | solution.py:396
  334.5 23.3 %collective-permute-start.3 = (bf16[2,64,1152]{2,1,0:T(8,128)(2,1)}, bf16[2,64,1152]{2,1,0:T(8,128)(2,1)}, u32[]{:S(2)}, u32[]{:S(2)}) collective-permute-start(bf16[2,64,1152]{2,1,0:T(8,128)(2,1)} %reduce-scatter.5.cloned.1.call-done), channel_id=1, source_target_pairs={{0,0},{1,32},{2,64},{3,96},{4,128},{5,160},{6,192},{7,224},{32,1},... | collective-permute-start | bytes 884744 | tf_op jit(solution)/shard_map/ppermute | solution.py:396
  336.4 0.8 copy-start.14
  342.9 0.8 copy-start.15
  (3 other events, 2.2 us)
Sparse Core Ops, SparseCore 0:
  35.2 68.0 all-gather.4
  105.7 52.2 all-gather.2
  192.2 53.1 reduce-scatter.2
  247.9 86.5 reduce-scatter.4

commit v2 on v1

--- a/solution.py
+++ b/solution.py
@@ -14,6 +14,8 @@
 CUTS = 8
 BLOCKS = CUTS * PAIR
 SLOTS = BLOCKS * CAP
+EACH = PAIR * CAP
+ROOM = 8
 TILE = 16
 TILES = SLOTS // TILE
 STEP = 5
@@ -25,9 +27,13 @@
     return lax.broadcasted_iota(jnp.int32, shape, dim)
 
 
-def target_of(adapter, ordinal):
+def whole_target(adapter, ordinal):
     dest = ((adapter >> 1) & 7) * 4 + (adapter >> 4)
     return dest * SLOTS + (adapter & 1) * CAP + ordinal
+
+
+def cut_target(adapter, ordinal):
+    return adapter * CAP + ordinal
 
 
 def as_row(column):
@@ -35,14 +41,14 @@
     return jnp.sum(jnp.where(iota((n, n), 0) == iota((n, n), 1), column, 0), axis=0, keepdims=True)
 
 
-def target_row(adapter):
+def target_row(adapter, target_of):
     n = adapter.shape[0]
     row = as_row(adapter)
     same = (adapter == row) & (iota((n, n), 0) < iota((n, n), 1))
     return target_of(row, jnp.sum(same.astype(jnp.int32), axis=0, keepdims=True))
 
 
-def target_column(adapter):
+def target_column(adapter, target_of):
     n = adapter.shape[0]
     same = (adapter == as_row(adapter)) & (iota((n, n), 1) < iota((n, n), 0))
     return target_of(adapter, jnp.sum(same.astype(jnp.int32), axis=1, keepdims=True))
@@ -82,7 +88,7 @@
     def kernel(a_ref, *refs):
         ins, o_ref = refs[:-1], refs[-1]
         t = pl.program_id(0)
-        first = target_row(a_ref[...])
+        first = target_row(a_ref[...], whole_target)
         slot = slot_at(iota((count, n), 0), t)
         spots = jnp.concatenate(
             [slot == first + PAIR * CAP * (2 * t + near) for near in range(NEAR)], axis=1
@@ -118,7 +124,7 @@
 
     def kernel(a_ref, m_ref, *outs):
         t = pl.program_id(0)
-        first = target_column(a_ref[...])
+        first = target_column(a_ref[...], whole_target)
         slot = slot_at(iota((n, count), 1), t)
         spots = jnp.concatenate(
             [slot == first + PAIR * CAP * (2 * t + near) for near in range(NEAR)], axis=0
@@ -151,6 +157,74 @@
     )(adapter, moved)
 
 
+def place_slices(adapter, values, sources):
+    n, total = values.shape
+    width = total // CUTS
+    slots = sources // CUTS * SLOTS
+    groups = sources // CUTS
+
+    def kernel(a_ref, v_ref, o_ref, p_ref):
+        @pl.when(pl.program_id(0) == 0)
+        def _():
+            spot = iota((slots, n), 0) == target_row(a_ref[...], cut_target)
+            p_ref[...] = spot.astype(F32).astype(BF16)
+
+        for k in range(2):
+            moved = jnp.dot(
+                p_ref[...], v_ref[:, k * width : (k + 1) * width], preferred_element_type=F32
+            )
+            o_ref[k * groups : (k + 1) * groups] = moved.astype(BF16).reshape(groups, SLOTS, width)
+
+    return pl.pallas_call(
+        kernel,
+        grid=(CUTS // 2,),
+        in_specs=[
+            pl.BlockSpec((n, 1), lambda j: (0, 0)),
+            pl.BlockSpec((n, 2 * width), lambda j: (0, j)),
+        ],
+        out_specs=pl.BlockSpec((2 * groups, SLOTS, width), lambda j: (j, 0, 0)),
+        out_shape=jax.ShapeDtypeStruct((sources, SLOTS, width), BF16),
+        scratch_shapes=[pltpu.VMEM((slots, n), BF16)],
+        compiler_params=params(),
+        cost_estimate=cost(2 * slots * n * total, 2 * total * (n + slots)),
+    )(adapter, values)
+
+
+def collect_slices(adapter, moved):
+    n = adapter.shape[0]
+    sources, _, width = moved.shape
+    groups = sources // CUTS
+    slots = groups * SLOTS
+
+    def kernel(a_ref, m_ref, o_ref, p_ref):
+        @pl.when(pl.program_id(0) == 0)
+        def _():
+            spot = iota((n, slots), 1) == target_column(a_ref[...], cut_target)
+            p_ref[...] = spot.astype(F32).astype(BF16)
+
+        for k in range(2):
+            found = jnp.dot(
+                p_ref[...],
+                m_ref[k * groups : (k + 1) * groups].reshape(slots, width),
+                preferred_element_type=F32,
+            )
+            o_ref[:, k * width : (k + 1) * width] = found.astype(BF16)
+
+    return pl.pallas_call(
+        kernel,
+        grid=(CUTS // 2,),
+        in_specs=[
+            pl.BlockSpec((n, 1), lambda j: (0, 0)),
+            pl.BlockSpec((2 * groups, SLOTS, width), lambda j: (j, 0, 0)),
+        ],
+        out_specs=pl.BlockSpec((n, 2 * width), lambda j: (0, j)),
+        out_shape=jax.ShapeDtypeStruct((n, width * CUTS), BF16),
+        scratch_shapes=[pltpu.VMEM((n, slots), BF16)],
+        compiler_params=params(),
+        cost_estimate=cost(2 * slots * n * width * CUTS, 2 * width * CUTS * (n + slots)),
+    )(adapter, moved)
+
+
 def held_weights(w_ref, t):
     _, rank, width = w_ref.shape
     return w_ref[pl.ds(STEP * t, HELD)].reshape(HELD * rank, width)
@@ -167,7 +241,7 @@
         kernel,
         grid=(TILES,),
         in_specs=[spec(v.shape) for v in ins],
-        out_specs=pl.BlockSpec(out.shape, lambda t: (0, 0, 0)) if whole_out else spec(out.shape),
+        out_specs=pl.BlockSpec(out.shape, lambda t: (0,) * len(out.shape)) if whole_out else spec(out.shape),
         out_shape=out,
         scratch_shapes=scratch,
         compiler_params=params(),
@@ -175,12 +249,12 @@
     )(*ins)
 
 
-def sum_slices(part_ref, o_ref, factor):
+def total_of_slices(part_ref):
     half = SLOTS // 2
     total = part_ref[:, :half, :] + part_ref[:, half:, :]
     total = total + pltpu.roll(total, half // 2, 1)
     total = total + pltpu.roll(total, half // 4, 1)
-    o_ref[...] = (factor * jnp.concatenate([total, total], axis=1)).astype(BF16)
+    return total
 
 
 def keep_part(part_ref, t, part):
@@ -191,7 +265,7 @@
             part_ref[:, tile * TILE : (tile + 1) * TILE, :] = part
 
 
-def lowered_rows(rows, shrink):
+def lowered_part(rows, shrink):
     sources, _, width = rows.shape
     count, rank = sources * TILE, shrink.shape[1]
 
@@ -211,16 +285,59 @@
 
         @pl.when(t == TILES - 1)
         def _():
-            sum_slices(part_ref, o_ref, 1.0)
-
+            o_ref[...] = jnp.zeros_like(o_ref)
+            for p in range(CUTS):
+                o_ref[p, :, :EACH, :] = part_ref[:, EACH * p : EACH * (p + 1), :]
+
+    out = jax.ShapeDtypeStruct((CUTS, sources, ROOM, rank), F32)
     return by_tile(
         kernel,
         (rows, shrink),
-        jax.ShapeDtypeStruct((sources, SLOTS, rank), BF16),
+        out,
         [pltpu.VMEM((sources, SLOTS, rank), F32)],
         2 * TILES * count * HELD * rank * width,
         whole_out=True,
     )
+
+
+def lowered_sum(parts):
+    _, sources, _, rank = parts.shape
+
+    def kernel(p_ref, o_ref, held_ref):
+        total = p_ref[0]
+        for p in range(1, CUTS):
+            total = total + p_ref[p]
+        for k in range(CUTS):
+            held_ref[:, EACH * k : EACH * (k + 1), :] = total[:, :EACH, :]
+        o_ref[...] = held_ref[...].astype(BF16)
+
+    return pl.pallas_call(
+        kernel,
+        out_shape=jax.ShapeDtypeStruct((sources, SLOTS, rank), BF16),
+        scratch_shapes=[pltpu.VMEM((sources, SLOTS, rank), F32)],
+        compiler_params=params(),
+        cost_estimate=cost(parts.size, 4 * parts.size),
+        name="lowered_sum",
+    )(parts)
+
+
+def backward_join(owned, sources):
+    rank = owned.shape[1]
+
+    def kernel(b_ref, o_ref, held_ref):
+        owned_rows = b_ref[...].astype(F32).reshape(CUTS, sources, ROOM, rank)
+        for p in range(CUTS):
+            held_ref[:, EACH * p : EACH * (p + 1), :] = owned_rows[p][:, :EACH, :]
+        o_ref[...] = held_ref[...].astype(BF16)
+
+    return pl.pallas_call(
+        kernel,
+        out_shape=jax.ShapeDtypeStruct((sources, SLOTS, rank), BF16),
+        scratch_shapes=[pltpu.VMEM((sources, SLOTS, rank), F32)],
+        compiler_params=params(),
+        cost_estimate=cost(owned.size, 4 * owned.size),
+        name="backward_join",
+    )(owned)
 
 
 def backward_rows(rows, expand, split):
@@ -249,12 +366,13 @@
 
         @pl.when(t == TILES - 1)
         def _():
-            sum_slices(part_ref, o_ref, SCALE)
+            total = SCALE * total_of_slices(part_ref)[:, :ROOM, :]
+            o_ref[...] = total.reshape(1, sources * ROOM, 2 * rank).astype(BF16)
 
     return by_tile(
         kernel,
         (rows, expand),
-        jax.ShapeDtypeStruct((sources, SLOTS, 2 * rank), BF16),
+        jax.ShapeDtypeStruct((1, sources * ROOM, 2 * rank), BF16),
         [pltpu.VMEM((sources, SLOTS, 2 * rank), F32)],
         2 * TILES * count * HELD * rank * width,
         whole_out=True,
@@ -397,11 +515,11 @@
 
 
 def gathered(shard):
-    return lax.all_gather(swap(shard), "z", axis=0, tiled=True)
+    return lax.all_gather(shard, "z", axis=0, tiled=True)
 
 
 def summed(parts):
-    return swap(lax.psum_scatter(parts, "z", scatter_dimension=0, tiled=True))
+    return lax.psum_scatter(parts, "z", scatter_dimension=0, tiled=True)
 
 
 def body(tokens, adapter_index, query_cotangent, value_cotangent, shrink, query_expand, value_expand):
@@ -409,22 +527,29 @@
     local, kinds, rank, width = shrink.shape
     value_width = value_expand.shape[2]
 
+    whole_shrink = gathered(shrink.reshape(local, kinds * rank, width))
+    sent_tokens = place_slices(adapter_index, tokens, sources)
+    rows_tokens = exchange(sent_tokens)
+    own_expand = swap(jnp.concatenate([query_expand, value_expand], axis=2))
+    whole_expand = gathered(own_expand)
     sent_both = place(adapter_index, (query_cotangent, value_cotangent), sources)
     rows_both = exchange(sent_both)
-    whole_expand = gathered(jnp.concatenate([query_expand, value_expand], axis=2))
-    whole_shrink = gathered(shrink.reshape(local, kinds * rank, width))
-    sent_tokens = place(adapter_index, (tokens,), sources)
-    rows_tokens = exchange(sent_tokens)
-
-    backward = backward_rows(rows_both, whole_expand, width)
+
+    part = lowered_part(rows_tokens, whole_shrink)
+    parts = lax.all_to_all(part, PARTS, 0, 0, tiled=True)
+    lowered = lowered_sum(parts)
+    owned = backward_rows(rows_both, whole_expand, width)[0]
+    owned = lax.all_gather(owned, PARTS, axis=0, tiled=True)
+    backward = backward_join(owned, sources)
+
+    out_both = exchange(expand_rows(lowered, whole_expand, width))
+    grad_expand = summed(expand_gradient(lowered, rows_both, rank, width))
+    grad_expand = swap(grad_expand).astype(F32)
     out_tokens = exchange(token_rows(backward, whole_shrink))
     grad_shrink = summed(shrink_gradient(backward, rows_tokens)).astype(F32)
-    lowered = lowered_rows(rows_tokens, whole_shrink)
-    out_both = exchange(expand_rows(lowered, whole_expand, width))
-    grad_expand = summed(expand_gradient(lowered, rows_both, rank, width)).astype(F32)
-
-    (token_gradient,) = collect(adapter_index, out_tokens, (width,))
+
     query_delta, value_delta = collect(adapter_index, out_both, (width, value_width))
+    token_gradient = collect_slices(adapter_index, out_tokens)
     return (
         query_delta,
         value_delta,

time: 371 us -> 322 us (0.87)
  the two profiles are of different devices: /device:TPU:8 before, /device:TPU:7 now
where the time goes in v2:
time: 322 us; the launch traced here: 318 us
  waiting for transfers between devices  144 us (45%)
  blocking collectives  57.4 us (18%)
  starting transfers between devices  38.6 us (12%)
  Pallas kernels  35.7 us (11%)
  local copies, waits for them, and re-layouts  25.7 us (8%)
  between operations  14 us (4%)
    all_to_all x3, waiting for transfers between devices, exchange(): return lax.all_to_all(values, ROUTE, 0, 0, tiled=True)  120 us
    all_to_all x1, blocking collectives, exchange(): return lax.all_to_all(values, ROUTE, 0, 0, tiled=True)  45.4 us
    all_to_all x3, starting transfers between devices, exchange(): return lax.all_to_all(values, ROUTE, 0, 0, tiled=True)  29.3 us
    unnamed x47, local copies, waits for them, and re-layouts  24.2 us
    pallas_call x6, Pallas kernels, by_tile(): pl.pallas_call(kernel, grid=(TILES,), in_specs=[spec(v.shape) for v in in...  21.6 us
    all_gather x1, blocking collectives, body(): owned = lax.all_gather(owned, PARTS, axis=0, tiled=True)  12 us
    all_gather x2, waiting for transfers between devices, gathered(): return lax.all_gather(shard, 'z', axis=0, tiled=True)  9.89 us
    ppermute x2, waiting for transfers between devices, swap(): return lax.ppermute(values, SWAP, turns)  6.65 us
  transfers between devices with their start and end apart: 10, of which 6 were waited for; matrix products, arithmetic and copies ran while one was open for 1% of the time, Pallas kernels for 10%

profile of v2, /device:TPU:7, one launch (start us, length us, event | category | flops | bytes accessed | tf_op | source)
XLA Modules:
  0.0 318.4 jit_solution(4021505080665498062)
XLA Ops:
  10.3 1.7 shard_map.118
  12.0 45.4 %all_to_all.25.x_ref = bf16[32,48,1024]{2,1,0:T(8,128)(2,1)S(1)} all-to-all(bf16[32,48,1024]{2,1,0:T(8,128)(2,1)S(1)} %shard_map.118), channel_id=1, replica_groups=mesh['y'=4,'c'=2,'x'=4,'z'=8] {'y','c','x'}, dimensions={0} | all-to-all | bytes 6291456 | tf_op jit(solution)/shard_map/all_to_all | solution.py:509
  57.4 9.9 %all-gather.4.cloned.1.call-done.w_ref = bf16[16,128,1024]{2,1,0:T(8,128)(2,1)} async-done(((bf16[2,128,1024]{2,1,0:T(8,128)(2,1)}), bf16[16,128,1024]{2,1,0:T(8,128)(2,1)}) %all-gather.4.cloned.1.call-update) | async-done | bytes 4194320 | tf_op jit(solution)/shard_map/all_gather | solution.py:518
  67.3 2.2 copy-done.17
  69.5 3.6 %shard_map.119 = f32[8,32,8,128]{3,2,1,0:T(8,128)S(1)} custom-call(bf16[32,48,1024]{2,1,0:T(8,128)(2,1)S(1)} %all_to_all.25.x_ref, bf16[16,128,1024]{2,1,0:T(8,128)(2,1)S(1)} %copy-done.17), custom_call_target="tpu_custom_call" | custom-call | flops 2415919104 | bytes 8388608 | tf_op jit(solution)/shard_map/pallas_call | solution.py:240
  74.0 5.1 %all-to-all-start.1 = ((f32[8,32,8,128]{3,2,1,0:T(8,128)}), f32[8,32,8,128]{3,2,1,0:T(8,128)S(1)}, u32[]{:S(2)}, u32[]{:S(2)}) async-start(f32[8,32,8,128]{3,2,1,0:T(8,128)} %copy-done.14), calls=%async_computation.1 | async-start | bytes 2097152 | tf_op jit(solution)/shard_map/all_to_all | solution.py:539
  80.2 1.9 collective-permute-start
  82.1 6.6 %collective-permute-done = bf16[2,64,1152]{2,1,0:T(8,128)(2,1)S(1)} collective-permute-done((bf16[2,64,1152]{2,1,0:T(8,128)(2,1)S(1)}, bf16[2,64,1152]{2,1,0:T(8,128)(2,1)S(1)}, u32[]{:S(2)}, u32[]{:S(2)}) %collective-permute-start) | collective-permute-done | bytes 294944 | tf_op jit(solution)/shard_map/ppermute | solution.py:514
  91.1 3.0 shard_map.122
  94.2 1.7 copy-done.6
  95.9 6.5 %all-to-all-done.1.p_ref = f32[8,32,8,128]{3,2,1,0:T(8,128)S(1)} async-done(((f32[8,32,8,128]{3,2,1,0:T(8,128)}), f32[8,32,8,128]{3,2,1,0:T(8,128)S(1)}, u32[]{:S(2)}, u32[]{:S(2)}) %all-to-all-start.1) | async-done | bytes 1048608 | tf_op jit(solution)/shard_map/all_to_all | solution.py:539
  103.4 17.7 %all-to-all-start.3 = ((bf16[32,48,1152]{2,1,0:T(8,128)(2,1)}), bf16[32,48,1152]{2,1,0:T(8,128)(2,1)S(1)}, u32[]{:S(2)}, u32[]{:S(2)}) async-start(bf16[32,48,1152]{2,1,0:T(8,128)(2,1)} %copy-done.6), calls=%async_computation.3 | async-start | bytes 7077888 | tf_op jit(solution)/shard_map/all_to_all | solution.py:509
  123.2 41.1 %all-to-all-done.3.x_ref = bf16[32,48,1152]{2,1,0:T(8,128)(2,1)S(1)} async-done(((bf16[32,48,1152]{2,1,0:T(8,128)(2,1)}), bf16[32,48,1152]{2,1,0:T(8,128)(2,1)S(1)}, u32[]{:S(2)}, u32[]{:S(2)}) %all-to-all-start.3) | async-done | bytes 3538976 | tf_op jit(solution)/shard_map/all_to_all | solution.py:509
  165.3 3.9 %shard_map.127 = bf16[16,64,1152]{2,1,0:T(8,128)(2,1)S(1)} custom-call(bf16[32,48,128]{2,1,0:T(8,128)(2,1)S(1)} %copy-done.8, bf16[32,48,1152]{2,1,0:T(8,128)(2,1)S(1)} %all-to-all-done.3.x_ref), custom_call_target="tpu_custom_call" | custom-call | flops 1358954496 | bytes 6291456 | tf_op jit(solution)/shard_map/pallas_call | solution.py:240
  170.7 1.7 copy-done.1
  172.4 3.3 %shard_map.123 = bf16[1,256,128]{2,1,0:T(8,128)(2,1)S(1)} custom-call(bf16[32,48,1152]{2,1,0:T(8,128)(2,1)S(1)} %all-to-all-done.3.x_ref, bf16[16,64,1152]{2,1,0:T(8,128)(2,1)S(1)} %copy-done.1), custom_call_target="tpu_custom_call" | custom-call | flops 1358954496 | bytes 5963776 | tf_op jit(solution)/shard_map/pallas_call | solution.py:240
  175.7 12.0 %all-gather = bf16[1,2048,128]{2,1,0:T(8,128)(2,1)S(1)} all-gather(bf16[1,256,128]{2,1,0:T(8,128)(2,1)S(1)} %shard_map.123), channel_id=2, replica_groups=mesh['y'=4,'c'=2,'x'=4,'z'=8] {'y','c'}, dimensions={1}, use_global_device_ids=true | all-gather | bytes 589824 | tf_op jit(solution)/shard_map/all_gather | solution.py:542
  187.8 3.6 %shard_map.126 = bf16[16,128,1024]{2,1,0:T(8,128)(2,1)S(1)} custom-call(bf16[32,48,128]{2,1,0:T(8,128)(2,1)S(1)} %backward_join.1.b_ref, bf16[32,48,1024]{2,1,0:T(8,128)(2,1)S(1)} %copy-done.11), custom_call_target="tpu_custom_call" | custom-call | flops 2415919104 | bytes 7733248 | tf_op jit(solution)/shard_map/pallas_call | solution.py:240
  191.4 2.0 copy-done.3
  193.4 2.2 copy-done.18
  195.7 3.3 %shard_map.124 = bf16[32,48,1024]{2,1,0:T(8,128)(2,1)S(1)} custom-call(bf16[32,48,128]{2,1,0:T(8,128)(2,1)S(1)} %backward_join.1.b_ref, bf16[16,128,1024]{2,1,0:T(8,128)(2,1)S(1)} %copy-done.18), custom_call_target="tpu_custom_call" | custom-call | flops 2415919104 | bytes 7733248 | tf_op jit(solution)/shard_map/pallas_call | solution.py:240
  199.0 1.8 copy-done.12
  200.8 6.4 %all-to-all-start.4 = ((bf16[32,48,1024]{2,1,0:T(8,128)(2,1)}), bf16[32,48,1024]{2,1,0:T(8,128)(2,1)S(1)}, u32[]{:S(2)}, u32[]{:S(2)}) async-start(bf16[32,48,1024]{2,1,0:T(8,128)(2,1)} %copy-done.12), calls=%async_computation.4 | async-start | bytes 6291456 | tf_op jit(solution)/shard_map/all_to_all | solution.py:509
  207.2 1.7 copy-done.2
  208.9 4.0 %shard_map.120 = bf16[32,48,1152]{2,1,0:T(8,128)(2,1)} custom-call(bf16[32,48,128]{2,1,0:T(8,128)(2,1)S(1)} %copy-done.9, bf16[16,64,1152]{2,1,0:T(8,128)(2,1)S(1)} %copy-done.2), custom_call_target="tpu_custom_call" | custom-call | flops 1358954496 | bytes 6291456 | tf_op jit(solution)/shard_map/pallas_call | solution.py:240
  212.8 33.0 %all-to-all-done.4.m_ref = bf16[32,48,1024]{2,1,0:T(8,128)(2,1)S(1)} async-done(((bf16[32,48,1024]{2,1,0:T(8,128)(2,1)}), bf16[32,48,1024]{2,1,0:T(8,128)(2,1)S(1)}, u32[]{:S(2)}, u32[]{:S(2)}) %all-to-all-start.4) | async-done | bytes 3145760 | tf_op jit(solution)/shard_map/all_to_all | solution.py:509
  245.9 5.2 %all-to-all-start.2 = ((bf16[32,48,1152]{2,1,0:T(8,128)(2,1)}), bf16[32,48,1152]{2,1,0:T(8,128)(2,1)}, u32[]{:S(2)}, u32[]{:S(2)}) async-start(bf16[32,48,1152]{2,1,0:T(8,128)(2,1)} %shard_map.120), calls=%async_computation.2 | async-start | bytes 7077888 | tf_op jit(solution)/shard_map/all_to_all | solution.py:509
  251.1 2.1 collective-permute-start.1
  253.2 2.8 shard_map.125
  256.0 46.0 %all-to-all-done.2.m_ref = bf16[32,48,1152]{2,1,0:T(8,128)(2,1)} async-done(((bf16[32,48,1152]{2,1,0:T(8,128)(2,1)}), bf16[32,48,1152]{2,1,0:T(8,128)(2,1)}, u32[]{:S(2)}, u32[]{:S(2)}) %all-to-all-start.2) | async-done | bytes 3538976 | tf_op jit(solution)/shard_map/all_to_all | solution.py:509
  302.1 6.2 %shard_map.121 = (bf16[128,8192]{1,0:T(8,128)(2,1)}, bf16[128,1024]{1,0:T(8,128)(2,1)}) custom-call(s32[128,1]{1,0:T(8,128)S(1)} %copy-done.16, bf16[32,48,1152]{2,1,0:T(8,128)(2,1)} %all-to-all-done.2.m_ref), custom_call_target="tpu_custom_call" | custom-call | flops 1811939328 | bytes 5898240 | tf_op jit(solution)/shard_map/pallas_call | solution.py:146
  308.3 2.1 convert.1
  (57 shorter events, 14.6 us)
Async XLA Ops:
  7.2 60.1 %all-gather.4.cloned.1.call-start = ((), (), s32[]{:S(2)}) async-start(), calls=%async_computation.7 | async-start | bytes 4718592 | tf_op jit(solution)/shard_map/all_gather | solution.py:518
  8.7 1.6 copy-start.13
  10.3 79.2 %copy-start.15 = (s32[128,1]{1,0:T(8,128)}, s32[128,1]{1,0:T(8,128)S(1)}, u32[]{:S(2)}) copy-start(s32[128,1]{1,0:T(8,128)S(1)} %copy.18.a_ref) | copy-start | bytes 1540
  57.4 15.7 %copy-start.10 = (bf16[32,48,1024]{2,1,0:T(8,128)(2,1)}, bf16[32,48,1024]{2,1,0:T(8,128)(2,1)S(1)}, u32[]{:S(2)}) copy-start(bf16[32,48,1024]{2,1,0:T(8,128)(2,1)S(1)} %all_to_all.25.x_ref) | copy-start | bytes 9437188
  67.3 2.2 copy-start.17
  69.5 9.7 %copy-start.22 = (bf16[2,64,128]{2,1,0:T(8,128)(2,1)S(1)}, bf16[2,64,128]{2,1,0:T(8,128)(2,1)}, u32[]{:S(2)}) copy-start(bf16[2,64,128]{2,1,0:T(8,128)(2,1)} %param.13) | copy-start | bytes 98308
  69.5 20.0 %copy-start.20 = (bf16[128,1024]{1,0:T(8,128)(2,1)S(1)}, bf16[128,1024]{1,0:T(8,128)(2,1)}, u32[]{:S(2)}) copy-start(bf16[128,1024]{1,0:T(8,128)(2,1)} %refs_1_.1) | copy-start | bytes 786436
  73.1 1.0 copy-start.14
  74.0 28.3 %all-to-all-start.1 = ((f32[8,32,8,128]{3,2,1,0:T(8,128)}), f32[8,32,8,128]{3,2,1,0:T(8,128)S(1)}, u32[]{:S(2)}, u32[]{:S(2)}) async-start(f32[8,32,8,128]{3,2,1,0:T(8,128)} %copy-done.14), calls=%async_computation.1 | async-start | bytes 2097152 | tf_op jit(solution)/shard_map/all_to_all | solution.py:539
  79.2 91.5 %all-gather.6.cloned.1.call-start = ((), (), s32[]{:S(2)}) async-start(), calls=%async_computation.8 | async-start | bytes 2654208 | tf_op jit(solution)/shard_map/all_gather | solution.py:518
  80.2 8.6 %collective-permute-start = (bf16[2,64,1152]{2,1,0:T(8,128)(2,1)S(1)}, bf16[2,64,1152]{2,1,0:T(8,128)(2,1)S(1)}, u32[]{:S(2)}, u32[]{:S(2)}) collective-permute-start(bf16[2,64,1152]{2,1,0:T(8,128)(2,1)S(1)} %pad_maximum_fusion), channel_id=1, source_target_pairs={{0,0},{1,32},{2,64},{3,96},{4,128},{5,160},{6,192},{7,224},{32,1},... | collective-permute-start | bytes 884744 | tf_op jit(solution)/shard_map/ppermute | solution.py:514
  89.5 1.6 copy-start.19
  94.1 1.7 copy-start.6
  102.4 1.0 copy-start.4
  103.4 60.9 %all-to-all-start.3 = ((bf16[32,48,1152]{2,1,0:T(8,128)(2,1)}), bf16[32,48,1152]{2,1,0:T(8,128)(2,1)S(1)}, u32[]{:S(2)}, u32[]{:S(2)}) async-start(bf16[32,48,1152]{2,1,0:T(8,128)(2,1)} %copy-done.6), calls=%async_computation.3 | async-start | bytes 7077888 | tf_op jit(solution)/shard_map/all_to_all | solution.py:509
  121.0 130.0 %reduce-scatter.5.cloned.1.call-start = ((), (), s32[]{:S(2)}) async-start(), calls=%async_computation.10 | async-start | bytes 2654208 | tf_op jit(solution)/shard_map/reduce_scatter | solution.py:522
  121.1 1.2 copy-start.5
  122.5 0.7 copy-start.7
  164.3 1.0 copy-start.8
  169.2 1.4 copy-start
  170.7 137.6 %reduce-scatter.3.cloned.1.call-start = ((), (), s32[]{:S(2)}) async-start(), calls=%async_computation.9 | async-start | bytes 4718592 | tf_op jit(solution)/shard_map/reduce_scatter | solution.py:522
  170.7 1.7 copy-start.1
  172.4 15.4 %copy-start.11 = (bf16[32,48,1024]{2,1,0:T(8,128)(2,1)S(1)}, bf16[32,48,1024]{2,1,0:T(8,128)(2,1)}, u32[]{:S(2)}) copy-start(bf16[32,48,1024]{2,1,0:T(8,128)(2,1)} %copy-done.10) | copy-start | bytes 9437188
  191.4 2.0 copy-start.3
  193.4 2.2 copy-start.18
  199.0 1.8 copy-start.12
  200.8 6.4 %copy-start.9 = (bf16[32,48,128]{2,1,0:T(8,128)(2,1)S(1)}, bf16[32,48,128]{2,1,0:T(8,128)(2,1)}, u32[]{:S(2)}) copy-start(bf16[32,48,128]{2,1,0:T(8,128)(2,1)} %copy-done.7) | copy-start | bytes 1179652
  200.8 45.1 %all-to-all-start.4 = ((bf16[32,48,1024]{2,1,0:T(8,128)(2,1)}), bf16[32,48,1024]{2,1,0:T(8,128)(2,1)S(1)}, u32[]{:S(2)}, u32[]{:S(2)}) async-start(bf16[32,48,1024]{2,1,0:T(8,128)(2,1)} %copy-done.12), calls=%async_computation.4 | async-start | bytes 6291456 | tf_op jit(solution)/shard_map/all_to_all | solution.py:509
  207.2 1.7 copy-start.2
  212.8 40.4 %copy-start.16 = (s32[128,1]{1,0:T(8,128)S(1)}, s32[128,1]{1,0:T(8,128)}, u32[]{:S(2)}) copy-start(s32[128,1]{1,0:T(8,128)} %copy-done.15) | copy-start | bytes 1540
  245.9 56.2 %all-to-all-start.2 = ((bf16[32,48,1152]{2,1,0:T(8,128)(2,1)}), bf16[32,48,1152]{2,1,0:T(8,128)(2,1)}, u32[]{:S(2)}, u32[]{:S(2)}) async-start(bf16[32,48,1152]{2,1,0:T(8,128)(2,1)} %shard_map.120), calls=%async_computation.2 | async-start | bytes 7077888 | tf_op jit(solution)/shard_map/all_to_all | solution.py:509
  251.1 59.3 %collective-permute-start.1 = (bf16[2,64,1152]{2,1,0:T(8,128)(2,1)}, bf16[2,64,1152]{2,1,0:T(8,128)(2,1)S(1)}, u32[]{:S(2)}, u32[]{:S(2)}) collective-permute-start(bf16[2,64,1152]{2,1,0:T(8,128)(2,1)} %reduce-scatter.5.cloned.1.call-done), channel_id=1, source_target_pairs={{0,0},{1,32},{2,64},{3,96},{4,128},{5,160},{6,192},{7,224},{32,1},... | collective-permute-start | bytes 884744 | tf_op jit(solution)/shard_map/ppermute | solution.py:514
  (1 other events, 0.7 us)
Sparse Core Ops, SparseCore 0:
  9.8 57.4 all-gather.3
  89.6 52.8 all-gather.5
  170.8 35.1 reduce-scatter.4
  208.4 77.4 reduce-scatter.2

commit v3 on v1

v3 whole, which is shorter than its diff:
```python
import jax
import jax.numpy as jnp
from jax import lax
from jax.experimental import pallas as pl
from jax.experimental.pallas import tpu as pltpu
from jax.sharding import Mesh, PartitionSpec as P


SCALE = 0.5
F32 = jnp.float32
BF16 = jnp.bfloat16
CAP = 3
CUTS = 8
BLOCKS = 16
SLOTS = BLOCKS * CAP
TILE = 16
TILES = SLOTS // TILE
STEP = 5
HELD = STEP + 1


def iota(shape, dim):
    return lax.broadcasted_iota(jnp.int32, shape, dim)


def cut_target(adapter, ordinal):
    return adapter * CAP + ordinal


def as_row(column):
    n = column.shape[0]
    return jnp.sum(jnp.where(iota((n, n), 0) == iota((n, n), 1), column, 0), axis=0, keepdims=True)


def target_row(adapter):
    n = adapter.shape[0]
    row = as_row(adapter)
    same = (adapter == row) & (iota((n, n), 0) < iota((n, n), 1))
    return cut_target(row, jnp.sum(same.astype(jnp.int32), axis=0, keepdims=True))


def target_column(adapter):
    n = adapter.shape[0]
    same = (adapter == as_row(adapter)) & (iota((n, n), 1) < iota((n, n), 0))
    return cut_target(adapter, jnp.sum(same.astype(jnp.int32), axis=1, keepdims=True))


def row_block(rows, t):
    inner = (iota((rows, 128), 0) & (TILE - 1)) + t
    block = jnp.zeros((rows, 128), jnp.int32)
    for k in range(1, HELD):
        block = block + (inner >= CAP * k).astype(jnp.int32)
    return block


def pair_of(block, pair):
    half = (iota(block.shape, 1) >= 64).astype(jnp.int32)
    return block == 2 * pair + half


def params():
    return pltpu.CompilerParams(vmem_limit_bytes=40 << 20)


def cost(flops, moved):
    return pl.CostEstimate(flops=flops, bytes_accessed=moved, transcendentals=0)


def place(adapter, values, sources):
    n = adapter.shape[0]
    widths = [v.shape[1] // CUTS for v in values]
    total = sum(widths)
    groups = sources // CUTS
    slots = groups * SLOTS

    def kernel(a_ref, *refs):
        ins, o_ref, p_ref = refs[:-2], refs[-2], refs[-1]

        @pl.when(pl.program_id(0) == 0)
        def _():
            spot = iota((slots, n), 0) == target_row(a_ref[...])
            p_ref[...] = spot.astype(F32).astype(BF16)

        at = 0
        for v_ref, width in zip(ins, widths):
            for k in range(2):
                moved = jnp.dot(
                    p_ref[...], v_ref[:, k * width : (k + 1) * width], preferred_element_type=F32
                )
                moved = moved.astype(BF16).reshape(groups, SLOTS, width)
                o_ref[k * groups : (k + 1) * groups, :, at : at + width] = moved
            at += width

    return pl.pallas_call(
        kernel,
        grid=(CUTS // 2,),
        in_specs=[pl.BlockSpec((n, 1), lambda j: (0, 0))]
        + [pl.BlockSpec((n, 2 * width), lambda j: (0, j)) for width in widths],
        out_specs=pl.BlockSpec((2 * groups, SLOTS, total), lambda j: (j, 0, 0)),
        out_shape=jax.ShapeDtypeStruct((sources, SLOTS, total), BF16),
        scratch_shapes=[pltpu.VMEM((slots, n), BF16)],
        compiler_params=params(),
        cost_estimate=cost(2 * slots * n * total * CUTS, 2 * total * CUTS * (n + slots)),
    )(adapter, *values)


def collect(adapter, moved, widths):
    n = adapter.shape[0]
    sources, _, total = moved.shape
    groups = sources // CUTS
    slots = groups * SLOTS

    def kernel(a_ref, m_ref, *refs):
        outs, p_ref = refs[:-1], refs[-1]

        @pl.when(pl.program_id(0) == 0)
        def _():
            spot = iota((n, slots), 1) == target_column(a_ref[...])
            p_ref[...] = spot.astype(F32).astype(BF16)

        at = 0
        for o_ref, width in zip(outs, widths):
            for k in range(2):
                found = jnp.dot(
                    p_ref[...],
                    m_ref[k * groups : (k + 1) * groups, :, at : at + width].reshape(slots, width),
                    preferred_element_type=F32,
                )
                o_ref[:, k * width : (k + 1) * width] = found.astype(BF16)
            at += width

    return pl.pallas_call(
        kernel,
        grid=(CUTS // 2,),
        in_specs=[
            pl.BlockSpec((n, 1), lambda j: (0, 0)),
            pl.BlockSpec((2 * groups, SLOTS, total), lambda j: (j, 0, 0)),
        ],
        out_specs=[pl.BlockSpec((n, 2 * width), lambda j: (0, j)) for width in widths],
        out_shape=[jax.ShapeDtypeStruct((n, width * CUTS), BF16) for width in widths],
        scratch_shapes=[pltpu.VMEM((n, slots), BF16)],
        compiler_params=params(),
        cost_estimate=cost(2 * slots * n * total * CUTS, 2 * total * CUTS * (n + slots)),
    )(adapter, moved)


def held_weights(w_ref, t):
    _, rank, width = w_ref.shape
    return w_ref[pl.ds(STEP * t, HELD)].reshape(HELD * rank, width)


def by_tile(kernel, ins, out, scratch, flops, whole_out=False):
    def spec(shape):
        if shape[1] == SLOTS:
            return pl.BlockSpec((shape[0], TILE, shape[2]), lambda t: (0, t, 0))
        return pl.BlockSpec(shape, lambda t: (0, 0, 0))

    moved = sum(v.size * v.dtype.itemsize for v in ins) + out.size * out.dtype.itemsize
    return pl.pallas_call(
        kernel,
        grid=(TILES,),
        in_specs=[spec(v.shape) for v in ins],
        out_specs=pl.BlockSpec(out.shape, lambda t: (0,) * len(out.shape)) if whole_out else spec(out.shape),
        out_shape=out,
        scratch_shapes=scratch,
        compiler_params=params(),
        cost_estimate=cost(flops, moved),
    )(*ins)


def lowered_part(rows, shrink):
    sources, _, width = rows.shape
    count, rank = sources * TILE, shrink.shape[1]

    def kernel(x_ref, w_ref, o_ref):
        t = pl.program_id(0)
        dense = lax.dot_general(
            x_ref[...].reshape(count, width),
            held_weights(w_ref, t),
            (((1,), (1,)), ((), ())),
            preferred_element_type=F32,
        )
        block = row_block(count, t)
        total = jnp.zeros((count, rank), F32)
        for b in range(HELD):
            total = total + jnp.where(block == b, dense[:, b * rank : (b + 1) * rank], 0.0)
        o_ref[...] = total.reshape(sources, TILE, rank)

    return by_tile(
        kernel,
        (rows, shrink),
        jax.ShapeDtypeStruct((sources, SLOTS, rank), F32),
        [],
        2 * TILES * count * HELD * rank * width,
    )


def backward_part(rows, expand, split):
    sources, _, width = rows.shape
    count, rank = sources * TILE, expand.shape[1]

    def kernel(x_ref, w_ref, o_ref):
        t = pl.program_id(0)
        x = x_ref[...].reshape(count, width)
        w = held_weights(w_ref, t)
        block = row_block(count, t)

        def part(lo, hi):
            dense = lax.dot_general(
                x[:, lo:hi], w[:, lo:hi], (((1,), (1,)), ((), ())), preferred_element_type=F32
            )
            total = jnp.zeros((count, 2 * rank), F32)
            for p in range(HELD // 2):
                piece = dense[:, 2 * rank * p : 2 * rank * (p + 1)]
                total = total + jnp.where(pair_of(block, p), piece, 0.0)
            return total + pltpu.roll(total, rank, 1)

        first = iota((count, 2 * rank), 1) < rank
        both = jnp.where(first, part(0, split), part(split, width))
        o_ref[...] = both.reshape(sources, TILE, 2 * rank)

    return by_tile(
        kernel,
        (rows, expand),
        jax.ShapeDtypeStruct((sources, SLOTS, 2 * rank), F32),
        [],
        2 * TILES * count * HELD * rank * width,
    )


def join_sums(low, back):
    parts, count, rank = low.shape

    def kernel(l_ref, b_ref, o_ref):
        for ref, factor, at in ((l_ref, 1.0, 0), (b_ref, SCALE, rank)):
            total = ref[0]
            for p in range(1, parts):
                total = total + ref[p]
            o_ref[:, at : at + rank] = (factor * total).astype(BF16)

    return pl.pallas_call(
        kernel,
        out_shape=jax.ShapeDtypeStruct((count, 2 * rank), BF16),
        compiler_params=params(),
        cost_estimate=cost(2 * low.size, 8 * low.size),
        name="join_sums",
    )(low, back)


def spread_pairs(values, count, rank, t):
    held = values.reshape(count, 2 * rank).astype(F32)
    turned = pltpu.roll(held, rank, 1)
    first = iota((count, 2 * rank), 1) < rank
    halves = (jnp.where(first, held, turned), jnp.where(first, turned, held))
    block = row_block(count, t)
    return [
        jnp.concatenate(
            [jnp.where(pair_of(block, p), half, 0.0) for p in range(HELD // 2)], axis=1
        ).astype(BF16)
        for half in halves
    ]


def spread_blocks(values, count, rank, t):
    held = values.reshape(count, rank).astype(F32)
    block = row_block(count, t)
    return jnp.concatenate(
        [jnp.where(block == b, held, 0.0) for b in range(HELD)], axis=1
    ).astype(BF16)


def expand_rows(joint, expand, split):
    sources = joint.shape[0]
    count, rank, width = sources * TILE, expand.shape[1], expand.shape[2]

    def kernel(l_ref, w_ref, o_ref):
        t = pl.program_id(0)
        w = held_weights(w_ref, t)
        halves = spread_pairs(l_ref[:, :, : 2 * rank], count, rank, t)
        for half, lo, hi in zip(halves, (0, split), (split, width)):
            result = SCALE * jnp.dot(half, w[:, lo:hi], preferred_element_type=F32)
            o_ref[:, :, lo:hi] = result.astype(BF16).reshape(sources, TILE, hi - lo)

    return by_tile(
        kernel,
        (joint, expand),
        jax.ShapeDtypeStruct((sources, SLOTS, width), BF16),
        [],
        2 * TILES * count * HELD * rank * width,
    )


def token_rows(joint, shrink):
    sources = joint.shape[0]
    count, rank, width = sources * TILE, shrink.shape[1], shrink.shape[2]

    def kernel(b_ref, w_ref, o_ref):
        t = pl.program_id(0)
        wide = spread_blocks(b_ref[:, :, rank:], count, rank, t)
        result = jnp.dot(wide, held_weights(w_ref, t), preferred_element_type=F32)
        o_ref[...] = result.astype(BF16).reshape(sources, TILE, width)

    return by_tile(
        kernel,
        (joint, shrink),
        jax.ShapeDtypeStruct((sources, SLOTS, width), BF16),
        [],
        2 * TILES * count * HELD * rank * width,
    )


def add_carry(carry_ref, pieces, rank, lo, hi):
    t = pl.program_id(0)
    first = pieces[:rank] + jnp.where(t > 0, carry_ref[:, lo:hi], 0.0)
    carry_ref[:, lo:hi] = pieces[STEP * rank :]
    done = jnp.concatenate([first, pieces[rank : STEP * rank]], axis=0)
    return done.astype(BF16).reshape(STEP, rank, hi - lo)


def fold(piece, width):
    narrow = piece.shape[-1]
    return jnp.concatenate([piece[..., 8 * i : 8 * i + 8, :] for i in range(width // narrow)], axis=-1)


def gradients(joint, rows_tokens, rows_both, split):
    sources, _, both = rows_both.shape
    count, pair = sources * TILE, joint.shape[2] // 2
    rank = pair // 2
    height = pair + rank + 8

    def put(o_ref, at, size, begin, end, value):
        o_ref[pl.ds(at, size), begin:end, :] = value

    def kernel(j_ref, t_ref, x_ref, o_ref, shrink_ref, expand_ref):
        t = pl.program_id(0)
        turn = (((0,), (0,)), ((), ()))
        wide = spread_blocks(j_ref[:, :, pair:], count, pair, t)
        tokens = t_ref[...].reshape(count, split)
        pieces = lax.dot_general(wide, tokens, turn, preferred_element_type=F32)
        put(o_ref, STEP * t, STEP, 0, pair, add_carry(shrink_ref, pieces, pair, 0, split))

        x = x_ref[...].reshape(count, both)
        halves = spread_pairs(j_ref[:, :, :pair], count, rank, t)
        pieces = SCALE * lax.dot_general(halves[0], x[:, :split], turn, preferred_element_type=F32)
        put(o_ref, STEP * t, STEP, pair, pair + rank, add_carry(expand_ref, pieces, rank, 0, split))
        pieces = SCALE * lax.dot_general(halves[1], x[:, split:], turn, preferred_element_type=F32)
        first = pieces[:rank] + jnp.where(t > 0, expand_ref[:, split:], 0.0)
        expand_ref[:, split:] = pieces[STEP * rank :]
        for b in range(STEP):
            piece = first if b == 0 else pieces[b * rank : (b + 1) * rank]
            o_ref[STEP * t + b, pair + rank :, :] = fold(piece, split).astype(BF16)

        @pl.when(t == TILES - 1)
        def _():
            o_ref[BLOCKS - 1, :pair, :] = shrink_ref[...].astype(BF16)
            o_ref[BLOCKS - 1, pair : pair + rank, :] = expand_ref[:, :split].astype(BF16)
            o_ref[BLOCKS - 1, pair + rank :, :] = fold(expand_ref[:, split:], split).astype(BF16)

    return by_tile(
        kernel,
        (joint, rows_tokens, rows_both),
        jax.ShapeDtypeStruct((BLOCKS, height, split), BF16),
        [pltpu.VMEM((pair, split), F32), pltpu.VMEM((rank, both), F32)],
        2 * TILES * count * HELD * (pair * split + rank * both),
        whole_out=True,
    )


def unpack(sums, rank, narrow):
    local, _, width = sums.shape
    pair = 2 * rank

    def kernel(g_ref, s_ref, q_ref, v_ref):
        s_ref[...] = g_ref[:, :pair, :].astype(F32)
        q_ref[...] = g_ref[:, pair : pair + rank, :].astype(F32)
        last = g_ref[:, pair + rank :, :].astype(F32)
        for i in range(width // narrow):
            v_ref[:, 8 * i : 8 * i + 8, :] = last[:, :, narrow * i : narrow * (i + 1)]

    return pl.pallas_call(
        kernel,
        out_shape=[
            jax.ShapeDtypeStruct((local, pair, width), F32),
            jax.ShapeDtypeStruct((local, rank, width), F32),
            jax.ShapeDtypeStruct((local, rank, narrow), F32),
        ],
        compiler_params=params(),
        cost_estimate=cost(sums.size, 6 * sums.size),
        name="unpack",
    )(sums)


ROUTE = ("y", "c", "x")
PARTS = ("y", "c")


def exchange(values):
    return lax.all_to_all(values, ROUTE, 0, 0, tiled=True)


def gathered(shard):
    return lax.all_gather(shard, "z", axis=0, tiled=True)


def summed(parts):
    return lax.psum_scatter(parts, "z", scatter_dimension=0, tiled=True)


def small_exchange(part):
    parts = lax.axis_size(PARTS)
    sources, slots, rank = part.shape
    return lax.all_to_all(part.reshape(parts, sources * slots // parts, rank), PARTS, 0, 0, tiled=True)


def body(tokens, adapter_index, query_cotangent, value_cotangent, shrink, query_expand, value_expand):
    sources = lax.axis_size(ROUTE)
    local, kinds, rank, width = shrink.shape
    value_width = value_expand.shape[2]

    whole_shrink = gathered(shrink.reshape(local, kinds * rank, width))
    sent_tokens = place(adapter_index, (tokens,), sources)
    rows_tokens = exchange(sent_tokens)
    whole_expand = gathered(jnp.concatenate([query_expand, value_expand], axis=2))
    sent_both = place(adapter_index, (query_cotangent, value_cotangent), sources)
    rows_both = exchange(sent_both)

    low = small_exchange(lowered_part(rows_tokens, whole_shrink))
    back = small_exchange(backward_part(rows_both, whole_expand, width))
    joint = lax.all_gather(join_sums(low, back), PARTS, axis=0, tiled=True)
    joint = joint.reshape(sources, SLOTS, 4 * rank)

    out_both = exchange(expand_rows(joint, whole_expand, width))
    sums = summed(gradients(joint, rows_tokens, rows_both, width))
    out_tokens = exchange(token_rows(joint, whole_shrink))

    query_delta, value_delta = collect(adapter_index, out_both, (width, value_width))
    (token_gradient,) = collect(adapter_index, out_tokens, (width,))
    grad_shrink, grad_query, grad_value = unpack(sums, rank, value_width)
    return (
        query_delta,
        value_delta,
        token_gradient,
        grad_shrink.reshape(local, kinds, rank, width),
        grad_query,
        grad_value,
    )


def solution(mesh):
    grid = Mesh(mesh.devices.reshape(4, 2, 4, 8), ("y", "c", "x", "z"))
    rows = P(("y", "c", "x", "z"), None)
    weights = (
        P(("x", "z"), None, None, PARTS),
        P(("x", "z"), None, PARTS),
        P(("x", "z"), None, PARTS),
    )

    return jax.shard_map(
        body,
        mesh=grid,
        in_specs=(rows, rows, rows, rows) + weights,
        out_specs=(rows, rows, rows) + weights,
        check_vma=False,
    )
```

time: 371 us -> 287 us (0.77)
  the two profiles are of different devices: /device:TPU:8 before, /device:TPU:7 now
where the time goes in v3:
time: 287 us; the launch traced here: 285 us
  waiting for transfers between devices  142 us (49%)
  local copies, waits for them, and re-layouts  34.7 us (12%)
  Pallas kernels  32.3 us (11%)
  blocking collectives  30.8 us (11%)
  starting transfers between devices  29.4 us (10%)
  between operations  14 us (5%)
    all_to_all x4, waiting for transfers between devices, exchange(): return lax.all_to_all(values, ROUTE, 0, 0, tiled=True)  139 us
    unnamed x49, local copies, waits for them, and re-layouts  34.7 us
    all_to_all x4, starting transfers between devices, exchange(): return lax.all_to_all(values, ROUTE, 0, 0, tiled=True)  25.1 us
    pallas_call x5, Pallas kernels, by_tile(): pl.pallas_call(kernel, grid=(TILES,), in_specs=[spec(v.shape) for v in in...  20.7 us
    all_to_all x1, blocking collectives, small_exchange(): lax.all_to_all(part.reshape(parts, sources * slots // parts, rank), PARTS...  16.5 us
    all_gather x1, blocking collectives, body(): joint = lax.all_gather(join_sums(low, back), PARTS, axis=0, tiled=True)  14.3 us
  transfers between devices with their start and end apart: 8, of which 5 were waited for; matrix products, arithmetic and copies ran while one was open for 0% of the time, Pallas kernels for 8%

profile of v3, /device:TPU:7, one launch (start us, length us, event | category | flops | bytes accessed | tf_op | source)
XLA Modules:
  0.0 285.4 jit_solution(17869053545955546001)
XLA Ops:
  7.2 1.7 pad_maximum_fusion
  13.0 1.9 shard_map.120
  14.9 1.7 copy-done.2
  16.6 7.9 %all-to-all-start.2 = ((bf16[32,48,1152]{2,1,0:T(8,128)(2,1)}), bf16[32,48,1152]{2,1,0:T(8,128)(2,1)S(1)}, u32[]{:S(2)}, u32[]{:S(2)}) async-start(bf16[32,48,1152]{2,1,0:T(8,128)(2,1)} %copy-done.2), calls=%async_computation.2 | async-start | bytes 7077888 | tf_op jit(solution)/shard_map/all_to_all | solution.py:398
  26.9 1.7 shard_map.118
  28.7 1.7 copy-done.5
  30.4 37.3 %all-to-all-done.2.x_ref = bf16[32,48,1152]{2,1,0:T(8,128)(2,1)S(1)} async-done(((bf16[32,48,1152]{2,1,0:T(8,128)(2,1)}), bf16[32,48,1152]{2,1,0:T(8,128)(2,1)S(1)}, u32[]{:S(2)}, u32[]{:S(2)}) %all-to-all-start.2) | async-done | bytes 3538976 | tf_op jit(solution)/shard_map/all_to_all | solution.py:398
  67.8 5.2 %all-to-all-start = ((bf16[32,48,1024]{2,1,0:T(8,128)(2,1)}), bf16[32,48,1024]{2,1,0:T(8,128)(2,1)}, u32[]{:S(2)}, u32[]{:S(2)}) async-start(bf16[32,48,1024]{2,1,0:T(8,128)(2,1)} %copy-done.5), calls=%async_computation | async-start | bytes 6291456 | tf_op jit(solution)/shard_map/all_to_all | solution.py:398
  73.0 1.7 copy-done.6
  74.7 3.2 %shard_map.121 = f32[32,48,128]{2,1,0:T(8,128)S(1)} custom-call(bf16[32,48,1152]{2,1,0:T(8,128)(2,1)S(1)} %all-to-all-done.2.x_ref, bf16[16,64,1152]{2,1,0:T(8,128)(2,1)S(1)} %copy-done.6), custom_call_target="tpu_custom_call" | custom-call | flops 1358954496 | bytes 6684672 | tf_op jit(solution)/shard_map/pallas_call | solution.py:159
  78.8 32.9 %all-to-all-done.x_ref.t_ref = bf16[32,48,1024]{2,1,0:T(8,128)(2,1)} async-done(((bf16[32,48,1024]{2,1,0:T(8,128)(2,1)}), bf16[32,48,1024]{2,1,0:T(8,128)(2,1)}, u32[]{:S(2)}, u32[]{:S(2)}) %all-to-all-start) | async-done | bytes 3145760 | tf_op jit(solution)/shard_map/all_to_all | solution.py:398
  111.7 4.2 %all-to-all-start.3 = ((f32[8,192,128]{2,1,0:T(8,128)}), f32[8,192,128]{2,1,0:T(8,128)}, u32[]{:S(2)}, u32[]{:S(2)}) async-start(f32[8,192,128]{2,1,0:T(8,128)} %bitcast.8), calls=%async_computation.3 | async-start | bytes 1572864 | tf_op jit(solution)/shard_map/all_to_all | solution.py:412
  115.9 2.2 copy-done.22
  118.1 4.6 %shard_map.119 = f32[32,48,128]{2,1,0:T(8,128)S(1)} custom-call(bf16[32,48,1024]{2,1,0:T(8,128)(2,1)} %all-to-all-done.x_ref.t_ref, bf16[16,128,1024]{2,1,0:T(8,128)(2,1)S(1)} %copy-done.22), custom_call_target="tpu_custom_call" | custom-call | flops 2415919104 | bytes 8126464 | tf_op jit(solution)/shard_map/pallas_call | solution.py:159
  123.6 2.9 %all-to-all-done.3.b_ref = f32[8,192,128]{2,1,0:T(8,128)} async-done(((f32[8,192,128]{2,1,0:T(8,128)}), f32[8,192,128]{2,1,0:T(8,128)}, u32[]{:S(2)}, u32[]{:S(2)}) %all-to-all-start.3) | async-done | bytes 786464 | tf_op jit(solution)/shard_map/all_to_all | solution.py:412
  126.5 16.5 %all_to_all.30.l_ref = f32[8,192,128]{2,1,0:T(8,128)S(1)} all-to-all(f32[8,192,128]{2,1,0:T(8,128)} %bitcast.9), channel_id=1, replica_groups=mesh['y'=4,'c'=2,'x'=4,'z'=8] {'y','c'}, dimensions={0} | all-to-all | bytes 1572864 | tf_op jit(solution)/shard_map/all_to_all | solution.py:412
  144.2 14.3 %all_gather.11 = bf16[1536,256]{1,0:T(8,128)(2,1)S(1)} all-gather(bf16[192,256]{1,0:T(8,128)(2,1)S(1)} %join_sums.1), channel_id=1, replica_groups=mesh['y'=4,'c'=2,'x'=4,'z'=8] {'y','c'}, dimensions={0}, use_global_device_ids=true | all-gather | bytes 884736 | tf_op jit(solution)/shard_map/all_gather | solution.py:429
  158.5 6.5 %shard_map.126 = bf16[16,200,1024]{2,1,0:T(8,128)(2,1)S(1)} custom-call(bf16[32,48,256]{2,1,0:T(8,128)(2,1)S(1)} %bitcast.5, bf16[32,48,1024]{2,1,0:T(8,128)(2,1)} %all-to-all-done.x_ref.t_ref, bf16[32,48,1152]{2,1,0:T(8,128)(2,1)S(1)} %all-to-all-done.2.x_ref), custom_call_target="tpu_custom_call" | custom-call | flops 3774873600 | bytes 14024704 | tf_op jit(solution)/shard_map/pallas_call | solution.py:159
  165.0 2.8 copy-done
  169.8 2.2 copy-done.23
  172.0 3.3 %shard_map.124 = bf16[32,48,1024]{2,1,0:T(8,128)(2,1)S(1)} custom-call(bf16[32,48,256]{2,1,0:T(8,128)(2,1)S(1)} %bitcast.6, bf16[16,128,1024]{2,1,0:T(8,128)(2,1)S(1)} %copy-done.23), custom_call_target="tpu_custom_call" | custom-call | flops 2415919104 | bytes 8126464 | tf_op jit(solution)/shard_map/pallas_call | solution.py:159
  175.3 1.8 copy-done.12
  177.1 7.0 %all-to-all-start.5 = ((bf16[32,48,1024]{2,1,0:T(8,128)(2,1)}), bf16[32,48,1024]{2,1,0:T(8,128)(2,1)S(1)}, u32[]{:S(2)}, u32[]{:S(2)}) async-start(bf16[32,48,1024]{2,1,0:T(8,128)(2,1)} %copy-done.12), calls=%async_computation.5 | async-start | bytes 6291456 | tf_op jit(solution)/shard_map/all_to_all | solution.py:398
  186.8 3.1 %shard_map.122 = bf16[32,48,1152]{2,1,0:T(8,128)(2,1)S(1)} custom-call(bf16[32,48,256]{2,1,0:T(8,128)(2,1)S(1)} %bitcast.7, bf16[16,64,1152]{2,1,0:T(8,128)(2,1)S(1)} %copy-done.7), custom_call_target="tpu_custom_call" | custom-call | flops 1358954496 | bytes 6684672 | tf_op jit(solution)/shard_map/pallas_call | solution.py:159
  189.9 1.8 copy-done.1
  191.8 30.9 %all-to-all-done.5.m_ref = bf16[32,48,1024]{2,1,0:T(8,128)(2,1)S(1)} async-done(((bf16[32,48,1024]{2,1,0:T(8,128)(2,1)}), bf16[32,48,1024]{2,1,0:T(8,128)(2,1)S(1)}, u32[]{:S(2)}, u32[]{:S(2)}) %all-to-all-start.5) | async-done | bytes 3145760 | tf_op jit(solution)/shard_map/all_to_all | solution.py:398
  222.7 1.8 copy-done.3
  224.5 5.1 %all-to-all-start.4 = ((bf16[32,48,1152]{2,1,0:T(8,128)(2,1)}), bf16[32,48,1152]{2,1,0:T(8,128)(2,1)S(1)}, u32[]{:S(2)}, u32[]{:S(2)}) async-start(bf16[32,48,1152]{2,1,0:T(8,128)(2,1)} %copy-done.1), calls=%async_computation.4 | async-start | bytes 7077888 | tf_op jit(solution)/shard_map/all_to_all | solution.py:398
  229.6 1.9 copy-done.4
  232.4 2.8 shard_map.125
  235.2 37.7 %all-to-all-done.4.m_ref = bf16[32,48,1152]{2,1,0:T(8,128)(2,1)S(1)} async-done(((bf16[32,48,1152]{2,1,0:T(8,128)(2,1)}), bf16[32,48,1152]{2,1,0:T(8,128)(2,1)S(1)}, u32[]{:S(2)}, u32[]{:S(2)}) %all-to-all-start.4) | async-done | bytes 3538976 | tf_op jit(solution)/shard_map/all_to_all | solution.py:398
  273.7 2.8 shard_map.123
  (50 shorter events, 18.4 us)
Async XLA Ops:
  7.2 65.8 %all-gather.5.cloned.1.call-start = ((), (), s32[]{:S(2)}) async-start(), calls=%async_computation.8 | async-start | bytes 2654208 | tf_op jit(solution)/shard_map/all_gather | solution.py:402
  8.9 106.9 %all-gather.3.cloned.1.call-start = ((), (), s32[]{:S(2)}) async-start(), calls=%async_computation.7 | async-start | bytes 4718592 | tf_op jit(solution)/shard_map/all_gather | solution.py:402
  10.5 1.6 copy-start.13
  12.1 0.9 copy-start.21
  13.0 3.6 %copy-start.15 = (s32[128,1]{1,0:T(8,128)}, s32[128,1]{1,0:T(8,128)S(1)}, u32[]{:S(2)}) copy-start(s32[128,1]{1,0:T(8,128)S(1)} %copy.19.a_ref) | copy-start | bytes 1540
  14.9 1.7 copy-start.2
  16.6 51.1 %all-to-all-start.2 = ((bf16[32,48,1152]{2,1,0:T(8,128)(2,1)}), bf16[32,48,1152]{2,1,0:T(8,128)(2,1)S(1)}, u32[]{:S(2)}, u32[]{:S(2)}) async-start(bf16[32,48,1152]{2,1,0:T(8,128)(2,1)} %copy-done.2), calls=%async_computation.2 | async-start | bytes 7077888 | tf_op jit(solution)/shard_map/all_to_all | solution.py:398
  24.5 1.6 copy-start.14
  26.1 0.8 copy-start.16
  28.7 1.7 copy-start.5
  67.8 43.9 %all-to-all-start = ((bf16[32,48,1024]{2,1,0:T(8,128)(2,1)}), bf16[32,48,1024]{2,1,0:T(8,128)(2,1)}, u32[]{:S(2)}, u32[]{:S(2)}) async-start(bf16[32,48,1024]{2,1,0:T(8,128)(2,1)} %copy-done.5), calls=%async_computation | async-start | bytes 6291456 | tf_op jit(solution)/shard_map/all_to_all | solution.py:398
  73.0 1.7 copy-start.6
  77.9 0.9 copy-start.11
  111.7 14.8 %all-to-all-start.3 = ((f32[8,192,128]{2,1,0:T(8,128)}), f32[8,192,128]{2,1,0:T(8,128)}, u32[]{:S(2)}, u32[]{:S(2)}) async-start(f32[8,192,128]{2,1,0:T(8,128)} %bitcast.8), calls=%async_computation.3 | async-start | bytes 1572864 | tf_op jit(solution)/shard_map/all_to_all | solution.py:412
  115.8 160.7 %reduce-scatter.2.cloned.1.call-start = ((), (), s32[]{:S(2)}) async-start(), calls=%async_computation.9 | async-start | bytes 7372800 | tf_op jit(solution)/shard_map/reduce_scatter | solution.py:406
  115.9 2.2 copy-start.22
  122.7 0.9 copy-start.20
  165.0 2.8 copy-start
  167.8 0.9 copy-start.8
  168.6 1.1 copy-start.9
  169.8 2.2 copy-start.23
  175.3 1.8 copy-start.12
  177.1 45.6 %all-to-all-start.5 = ((bf16[32,48,1024]{2,1,0:T(8,128)(2,1)}), bf16[32,48,1024]{2,1,0:T(8,128)(2,1)S(1)}, u32[]{:S(2)}, u32[]{:S(2)}) async-start(bf16[32,48,1024]{2,1,0:T(8,128)(2,1)} %copy-done.12), calls=%async_computation.5 | async-start | bytes 6291456 | tf_op jit(solution)/shard_map/all_to_all | solution.py:398
  184.0 1.7 copy-start.7
  185.7 1.1 copy-start.10
  189.9 1.9 copy-start.1
  222.7 1.8 copy-start.3
  224.5 48.4 %all-to-all-start.4 = ((bf16[32,48,1152]{2,1,0:T(8,128)(2,1)}), bf16[32,48,1152]{2,1,0:T(8,128)(2,1)S(1)}, u32[]{:S(2)}, u32[]{:S(2)}) async-start(bf16[32,48,1152]{2,1,0:T(8,128)(2,1)} %copy-done.1), calls=%async_computation.4 | async-start | bytes 7077888 | tf_op jit(solution)/shard_map/all_to_all | solution.py:398
  229.6 1.9 copy-start.4
  231.6 0.8 copy-start.17
  272.9 0.8 copy-start.18
  276.5 1.1 copy-start.19
Sparse Core Ops, SparseCore 0:
  10.3 40.4 all-gather.4
  52.6 56.9 all-gather.2
  168.8 79.5 reduce-scatter.1

commit v4 on v3

--- a/solution.py
+++ b/solution.py
@@ -104,20 +104,28 @@
     )(adapter, *values)
 
 
-def collect(adapter, moved, widths):
+def find_slots(adapter, slots):
     n = adapter.shape[0]
+
+    def kernel(a_ref, o_ref):
+        spot = iota((n, slots), 1) == target_column(a_ref[...])
+        o_ref[...] = spot.astype(F32).astype(BF16)
+
+    return pl.pallas_call(
+        kernel,
+        out_shape=jax.ShapeDtypeStruct((n, slots), BF16),
+        compiler_params=params(),
+        cost_estimate=cost(n * slots, 2 * n * slots),
+        name="find_slots",
+    )(adapter)
+
+
+def collect(spots, moved, widths):
+    n, slots = spots.shape
     sources, _, total = moved.shape
     groups = sources // CUTS
-    slots = groups * SLOTS
-
-    def kernel(a_ref, m_ref, *refs):
-        outs, p_ref = refs[:-1], refs[-1]
-
-        @pl.when(pl.program_id(0) == 0)
-        def _():
-            spot = iota((n, slots), 1) == target_column(a_ref[...])
-            p_ref[...] = spot.astype(F32).astype(BF16)
-
+
+    def kernel(p_ref, m_ref, *outs):
         at = 0
         for o_ref, width in zip(outs, widths):
             for k in range(2):
@@ -133,15 +141,14 @@
         kernel,
         grid=(CUTS // 2,),
         in_specs=[
-            pl.BlockSpec((n, 1), lambda j: (0, 0)),
+            pl.BlockSpec((n, slots), lambda j: (0, 0)),
             pl.BlockSpec((2 * groups, SLOTS, total), lambda j: (j, 0, 0)),
         ],
         out_specs=[pl.BlockSpec((n, 2 * width), lambda j: (0, j)) for width in widths],
         out_shape=[jax.ShapeDtypeStruct((n, width * CUTS), BF16) for width in widths],
-        scratch_shapes=[pltpu.VMEM((n, slots), BF16)],
         compiler_params=params(),
         cost_estimate=cost(2 * slots * n * total * CUTS, 2 * total * CUTS * (n + slots)),
-    )(adapter, moved)
+    )(spots, moved)
 
 
 def held_weights(w_ref, t):
@@ -168,83 +175,87 @@
     )(*ins)
 
 
-def lowered_part(rows, shrink):
+def part_kernel(rows, weights, part, compute):
     sources, _, width = rows.shape
-    count, rank = sources * TILE, shrink.shape[1]
-
-    def kernel(x_ref, w_ref, o_ref):
+    count, columns = sources * TILE, 128
+    groups = sources // CUTS
+
+    def kernel(me_ref, x_ref, w_ref, *refs):
+        outs, held_ref = refs[:-1], refs[-1]
         t = pl.program_id(0)
-        dense = lax.dot_general(
-            x_ref[...].reshape(count, width),
-            held_weights(w_ref, t),
-            (((1,), (1,)), ((), ())),
-            preferred_element_type=F32,
-        )
-        block = row_block(count, t)
-        total = jnp.zeros((count, rank), F32)
+        total = compute(x_ref[...].reshape(count, width), held_weights(w_ref, t), row_block(count, t))
+        held_ref[...] = total.reshape(sources, TILE, columns)
+        for r in range(CUTS):
+            outs[r][...] = held_ref[pl.ds((me_ref[0] ^ r) * groups, groups)]
+
+    moved = 2 * (rows.size + weights.size) + 4 * sources * SLOTS * columns
+    return pl.pallas_call(
+        kernel,
+        grid=(TILES,),
+        in_specs=[
+            pl.BlockSpec(memory_space=pltpu.SMEM),
+            pl.BlockSpec((sources, TILE, width), lambda t: (0, t, 0)),
+            pl.BlockSpec(weights.shape, lambda t: (0, 0, 0)),
+        ],
+        out_specs=[pl.BlockSpec((groups, TILE, columns), lambda t: (0, t, 0))] * CUTS,
+        out_shape=[jax.ShapeDtypeStruct((groups, SLOTS, columns), F32)] * CUTS,
+        scratch_shapes=[pltpu.VMEM((sources, TILE, columns), F32)],
+        compiler_params=params(),
+        cost_estimate=cost(2 * TILES * count * HELD * weights.shape[1] * width, moved),
+    )(part, rows, weights)
+
+
+def lowered_part(rows, shrink, part):
+    rank = shrink.shape[1]
+
+    def compute(x, w, block):
+        dense = lax.dot_general(x, w, (((1,), (1,)), ((), ())), preferred_element_type=F32)
+        total = jnp.zeros((x.shape[0], rank), F32)
         for b in range(HELD):
             total = total + jnp.where(block == b, dense[:, b * rank : (b + 1) * rank], 0.0)
-        o_ref[...] = total.reshape(sources, TILE, rank)
-
-    return by_tile(
-        kernel,
-        (rows, shrink),
-        jax.ShapeDtypeStruct((sources, SLOTS, rank), F32),
-        [],
-        2 * TILES * count * HELD * rank * width,
-    )
-
-
-def backward_part(rows, expand, split):
-    sources, _, width = rows.shape
-    count, rank = sources * TILE, expand.shape[1]
-
-    def kernel(x_ref, w_ref, o_ref):
-        t = pl.program_id(0)
-        x = x_ref[...].reshape(count, width)
-        w = held_weights(w_ref, t)
-        block = row_block(count, t)
-
-        def part(lo, hi):
+        return total
+
+    return part_kernel(rows, shrink, part, compute)
+
+
+def backward_part(rows, expand, split, part):
+    width, rank = rows.shape[2], expand.shape[1]
+
+    def compute(x, w, block):
+        def half(lo, hi):
             dense = lax.dot_general(
                 x[:, lo:hi], w[:, lo:hi], (((1,), (1,)), ((), ())), preferred_element_type=F32
             )
-            total = jnp.zeros((count, 2 * rank), F32)
+            total = jnp.zeros((x.shape[0], 2 * rank), F32)
             for p in range(HELD // 2):
                 piece = dense[:, 2 * rank * p : 2 * rank * (p + 1)]
                 total = total + jnp.where(pair_of(block, p), piece, 0.0)
             return total + pltpu.roll(total, rank, 1)
 
-        first = iota((count, 2 * rank), 1) < rank
-        both = jnp.where(first, part(0, split), part(split, width))
-        o_ref[...] = both.reshape(sources, TILE, 2 * rank)
-
-    return by_tile(
-        kernel,
-        (rows, expand),
-        jax.ShapeDtypeStruct((sources, SLOTS, 2 * rank), F32),
-        [],
-        2 * TILES * count * HELD * rank * width,
-    )
+        first = iota((x.shape[0], 2 * rank), 1) < rank
+        return jnp.where(first, half(0, split), half(split, width))
+
+    return part_kernel(rows, expand, part, compute)
 
 
 def join_sums(low, back):
-    parts, count, rank = low.shape
-
-    def kernel(l_ref, b_ref, o_ref):
-        for ref, factor, at in ((l_ref, 1.0, 0), (b_ref, SCALE, rank)):
-            total = ref[0]
-            for p in range(1, parts):
-                total = total + ref[p]
-            o_ref[:, at : at + rank] = (factor * total).astype(BF16)
-
-    return pl.pallas_call(
-        kernel,
-        out_shape=jax.ShapeDtypeStruct((count, 2 * rank), BF16),
-        compiler_params=params(),
-        cost_estimate=cost(2 * low.size, 8 * low.size),
+    groups, slots, rank = low[0].shape
+
+    def kernel(*refs):
+        o_ref = refs[-1]
+        for at, factor in ((0, 1.0), (1, SCALE)):
+            total = refs[at * CUTS][...]
+            for ref in refs[at * CUTS + 1 : (at + 1) * CUTS]:
+                total = total + ref[...]
+            o_ref[:, :, at * rank : (at + 1) * rank] = (factor * total).astype(BF16)
+
+    return pl.pallas_call(
+        kernel,
+        out_shape=jax.ShapeDtypeStruct((groups, slots, 2 * rank), BF16),
+        compiler_params=params(),
+        cost_estimate=cost(2 * CUTS * low[0].size, 8 * CUTS * low[0].size),
         name="join_sums",
-    )(low, back)
+    )(*low, *back)
 
 
 def spread_pairs(values, count, rank, t):
@@ -269,25 +280,42 @@
     ).astype(BF16)
 
 
-def expand_rows(joint, expand, split):
-    sources = joint.shape[0]
+def expand_rows(pieces, part, expand, split):
+    groups, _, columns = pieces[0].shape
+    sources = groups * CUTS
     count, rank, width = sources * TILE, expand.shape[1], expand.shape[2]
 
-    def kernel(l_ref, w_ref, o_ref):
+    def kernel(me_ref, *refs):
+        ins, w_ref, o_ref, j_ref = refs[:CUTS], refs[CUTS], refs[-2], refs[-1]
         t = pl.program_id(0)
+        for r in range(CUTS):
+            j_ref[pl.ds((me_ref[0] ^ r) * groups, groups)] = ins[r][...]
         w = held_weights(w_ref, t)
-        halves = spread_pairs(l_ref[:, :, : 2 * rank], count, rank, t)
+        halves = spread_pairs(j_ref[:, :, : 2 * rank], count, rank, t)
         for half, lo, hi in zip(halves, (0, split), (split, width)):
             result = SCALE * jnp.dot(half, w[:, lo:hi], preferred_element_type=F32)
             o_ref[:, :, lo:hi] = result.astype(BF16).reshape(sources, TILE, hi - lo)
 
-    return by_tile(
-        kernel,
-        (joint, expand),
-        jax.ShapeDtypeStruct((sources, SLOTS, width), BF16),
-        [],
-        2 * TILES * count * HELD * rank * width,
-    )
+    return pl.pallas_call(
+        kernel,
+        grid=(TILES,),
+        in_specs=[pl.BlockSpec(memory_space=pltpu.SMEM)]
+        + [pl.BlockSpec((groups, TILE, columns), lambda t: (0, t, 0))] * CUTS
+        + [pl.BlockSpec(expand.shape, lambda t: (0, 0, 0))],
+        out_specs=[
+            pl.BlockSpec((sources, TILE, width), lambda t: (0, t, 0)),
+            pl.BlockSpec((sources, TILE, columns), lambda t: (0, t, 0)),
+        ],
+        out_shape=[
+            jax.ShapeDtypeStruct((sources, SLOTS, width), BF16),
+            jax.ShapeDtypeStruct((sources, SLOTS, columns), BF16),
+        ],
+        compiler_params=params(),
+        cost_estimate=cost(
+            2 * TILES * count * HELD * rank * width, 2 * (expand.size + sources * SLOTS * (width + 2 * columns))
+        ),
+        name="expand_rows",
+    )(part, *pieces, expand)
 
 
 def token_rows(joint, shrink):
@@ -406,10 +434,11 @@
     return lax.psum_scatter(parts, "z", scatter_dimension=0, tiled=True)
 
 
-def small_exchange(part):
-    parts = lax.axis_size(PARTS)
-    sources, slots, rank = part.shape
-    return lax.all_to_all(part.reshape(parts, sources * slots // parts, rank), PARTS, 0, 0, tiled=True)
+def to_partners(parts):
+    moved = [parts[0]]
+    for r in range(1, CUTS):
+        moved.append(lax.ppermute(parts[r], PARTS, [(i, i ^ r) for i in range(CUTS)]))
+    return moved
 
 
 def body(tokens, adapter_index, query_cotangent, value_cotangent, shrink, query_expand, value_expand):
@@ -424,17 +453,19 @@
     sent_both = place(adapter_index, (query_cotangent, value_cotangent), sources)
     rows_both = exchange(sent_both)
 
-    low = small_exchange(lowered_part(rows_tokens, whole_shrink))
-    back = small_exchange(backward_part(rows_both, whole_expand, width))
-    joint = lax.all_gather(join_sums(low, back), PARTS, axis=0, tiled=True)
-    joint = joint.reshape(sources, SLOTS, 4 * rank)
-
-    out_both = exchange(expand_rows(joint, whole_expand, width))
+    spots = find_slots(adapter_index, sources // CUTS * SLOTS)
+    me = jnp.reshape(lax.axis_index(PARTS), (1,)).astype(jnp.int32)
+    low = to_partners(lowered_part(rows_tokens, whole_shrink, me))
+    back = to_partners(backward_part(rows_both, whole_expand, width, me))
+    pieces = to_partners([join_sums(low, back)] * CUTS)
+
+    sent_both, joint = expand_rows(pieces, me, whole_expand, width)
+    out_both = exchange(sent_both)
     sums = summed(gradients(joint, rows_tokens, rows_both, width))
     out_tokens = exchange(token_rows(joint, whole_shrink))
 
-    query_delta, value_delta = collect(adapter_index, out_both, (width, value_width))
-    (token_gradient,) = collect(adapter_index, out_tokens, (width,))
+    query_delta, value_delta = collect(spots, out_both, (width, value_width))
+    (token_gradient,) = collect(spots, out_tokens, (width,))
     grad_shrink, grad_query, grad_value = unpack(sums, rank, value_width)
     return (
         query_delta,

time: 287 us -> 287 us (level)
  waiting for transfers between devices: 142 us -> 121 us
  starting transfers between devices: 29.4 us -> 42.8 us
  blocking collectives: 30.8 us -> 43.5 us
  local copies, waits for them, and re-layouts: 34.7 us -> 27.2 us
  Pallas kernels: 32.3 us -> 36.2 us
    all_to_all x4 -> x3, waiting for transfers between devices: 139 us -> 102 us  [exchange(): return lax.all_to_all(values, ROUTE, 0, 0, tiled=True)]
    all_to_all x1, blocking collectives: 16.5 us -> 43.5 us  [exchange(): return lax.all_to_all(values, ROUTE, 0, 0, tiled=True)]
    ppermute x0 -> x21, starting transfers between devices: none -> 23.1 us  [to_partners(): lax.ppermute(parts[r], PARTS, [(i, i ^ r) for i in range(CUTS)])]
    ppermute x0 -> x21, waiting for transfers between devices: none -> 18.4 us  [to_partners(): lax.ppermute(parts[r], PARTS, [(i, i ^ r) for i in range(CUTS)])]
    pallas_call x3 -> x7, Pallas kernels: 6.79 us -> 21.6 us  [the longest x2 8.87 us: part_kernel(): pl.pallas_call(kernel, grid=(TILES,), in_specs=[pl.BlockSpec(memory_space...]
    all_gather x1 -> x0, blocking collectives: 14.3 us -> none  [body(): joint = lax.all_gather(join_sums(low, back), PARTS, axis=0, tiled=True)]
    pallas_call x5 -> x2, Pallas kernels: 20.7 us -> 9.83 us  [by_tile(): pl.pallas_call(kernel, grid=(TILES,), in_specs=[spec(v.shape) for v in in...]
    unnamed x49 -> x51, local copies, waits for them, and re-layouts: 34.7 us -> 27.2 us
  transfers between devices with their start and end apart: 8 -> 27, of which waited for: 5 -> 12; matrix products, arithmetic and copies ran while one was open for 0% -> 0% of each run, Pallas kernels for 8% -> 8%
where the time goes in v4:
time: 287 us; the launch traced here: 286 us
  waiting for transfers between devices  121 us (42%)
  blocking collectives  43.5 us (15%)
  starting transfers between devices  42.8 us (15%)
  Pallas kernels  36.2 us (13%)
  local copies, waits for them, and re-layouts  27.2 us (9%)
  between operations  14 us (5%)
    all_to_all x3, waiting for transfers between devices, exchange(): return lax.all_to_all(values, ROUTE, 0, 0, tiled=True)  102 us
    all_to_all x1, blocking collectives, exchange(): return lax.all_to_all(values, ROUTE, 0, 0, tiled=True)  43.5 us
    unnamed x51, local copies, waits for them, and re-layouts  27.2 us
    ppermute x21, starting transfers between devices, to_partners(): lax.ppermute(parts[r], PARTS, [(i, i ^ r) for i in range(CUTS)])  23.1 us
    all_to_all x3, starting transfers between devices, exchange(): return lax.all_to_all(values, ROUTE, 0, 0, tiled=True)  19.6 us
    ppermute x21, waiting for transfers between devices, to_partners(): lax.ppermute(parts[r], PARTS, [(i, i ^ r) for i in range(CUTS)])  18.4 us
    pallas_call x2, Pallas kernels, by_tile(): pl.pallas_call(kernel, grid=(TILES,), in_specs=[spec(v.shape) for v in in...  9.83 us
    pallas_call x2, Pallas kernels, part_kernel(): pl.pallas_call(kernel, grid=(TILES,), in_specs=[pl.BlockSpec(memory_space...  8.87 us
  transfers between devices with their start and end apart: 27, of which 12 were waited for; matrix products, arithmetic and copies ran while one was open for 0% of the time, Pallas kernels for 8%

profile of v4, /device:TPU:7, one launch (start us, length us, event | category | flops | bytes accessed | tf_op | source)
XLA Modules:
  0.0 286.4 jit_solution(2260966572087449755)
XLA Ops:
  14.5 1.9 shard_map.120
  18.1 7.8 %all-to-all-start.1 = ((bf16[32,48,1152]{2,1,0:T(8,128)(2,1)}), bf16[32,48,1152]{2,1,0:T(8,128)(2,1)S(1)}, u32[]{:S(2)}, u32[]{:S(2)}) async-start(bf16[32,48,1152]{2,1,0:T(8,128)(2,1)} %copy-done.1), calls=%async_computation.1 | async-start | bytes 7077888 | tf_op jit(solution)/shard_map/all_to_all | solution.py:426
  31.9 37.4 %all-to-all-done.1.x_ref = bf16[32,48,1152]{2,1,0:T(8,128)(2,1)S(1)} async-done(((bf16[32,48,1152]{2,1,0:T(8,128)(2,1)}), bf16[32,48,1152]{2,1,0:T(8,128)(2,1)S(1)}, u32[]{:S(2)}, u32[]{:S(2)}) %all-to-all-start.1) | async-done | bytes 3538976 | tf_op jit(solution)/shard_map/all_to_all | solution.py:426
  69.2 5.2 %all-to-all-start = ((bf16[32,48,1024]{2,1,0:T(8,128)(2,1)}), bf16[32,48,1024]{2,1,0:T(8,128)(2,1)}, u32[]{:S(2)}, u32[]{:S(2)}) async-start(bf16[32,48,1024]{2,1,0:T(8,128)(2,1)} %copy-done.2), calls=%async_computation | async-start | bytes 6291456 | tf_op jit(solution)/shard_map/all_to_all | solution.py:426
  76.2 4.0 %shard_map.121 = (f32[4,48,128]{2,1,0:T(8,128)S(1)}, f32[4,48,128]{2,1,0:T(8,128)}, f32[4,48,128]{2,1,0:T(8,128)}, f32[4,48,128]{2,1,0:T(8,128)}, f32[4,48,128]{...) custom-call(s32[1]{0:T(128)} %bitcast.me_ref, ...), custom_call_target="tpu_custom_call" | custom-call | flops 1358954496 | bytes 6684672 | tf_op jit(solution)/shard_map/pallas_call | solution.py:192
  84.3 2.7 collective-permute-start.10
  87.5 25.7 %all-to-all-done.x_ref.t_ref = bf16[32,48,1024]{2,1,0:T(8,128)(2,1)} async-done(((bf16[32,48,1024]{2,1,0:T(8,128)(2,1)}), bf16[32,48,1024]{2,1,0:T(8,128)(2,1)}, u32[]{:S(2)}, u32[]{:S(2)}) %all-to-all-start) | async-done | bytes 3145760 | tf_op jit(solution)/shard_map/all_to_all | solution.py:426
  113.2 2.2 copy-done.19
  115.4 4.8 %shard_map.119 = (f32[4,48,128]{2,1,0:T(8,128)S(1)}, f32[4,48,128]{2,1,0:T(8,128)S(1)}, f32[4,48,128]{2,1,0:T(8,128)S(1)}, f32[4,48,128]{2,1,0:T(8,128)S(1)}, f3...) custom-call(s32[1]{0:T(128)} %bitcast.me_ref, ...), custom_call_target="tpu_custom_call" | custom-call | flops 2415919104 | bytes 8126464 | tf_op jit(solution)/shard_map/pallas_call | solution.py:192
  121.6 1.9 collective-permute-start
  125.3 2.0 collective-permute-done.13.refs_15_
  128.5 1.8 collective-permute-start.5
  132.3 2.5 collective-permute-done.4.refs_5_
  134.7 2.2 collective-permute-done.5.refs_6_
  137.0 2.1 collective-permute-done.6.refs_7_
  140.9 1.7 collective-permute-start.16
  145.9 2.1 collective-permute-start.19
  148.9 2.3 collective-permute-done.17.refs_4_
  151.2 2.5 collective-permute-done.18.refs_5_
  153.6 1.8 collective-permute-done.19.refs_6_
  155.5 2.1 collective-permute-done.20.refs_7_
  157.6 4.2 %expand_rows.1 = (bf16[32,48,1152]{2,1,0:T(8,128)(2,1)}, bf16[32,48,256]{2,1,0:T(8,128)(2,1)S(1)}) custom-call(s32[1]{0:T(128)} %bitcast.me_ref, bf16[4,48,256]{2,1,0:T(8,128)(2,1)S(1)} %join_sums.1.refs_0_, bf16[4,48,256]{2,1,0:T(8,128)(2,1)S(1)} %collective-permute-done.14.refs_1_, bf16[4,48,256]{2,1,0:T(8,128)(2,1)S(1)} %collective-permute-done.15.refs_2_, ...), custom_call_target="tpu_custom_call" | custom-call | flops 1358954496 | bytes 7471104 | tf_op jit(solution)/shard_map/expand_rows/pallas_call | solution.py:299
  161.8 6.5 %shard_map.125 = bf16[16,200,1024]{2,1,0:T(8,128)(2,1)S(1)} custom-call(bf16[32,48,256]{2,1,0:T(8,128)(2,1)S(1)} %get-tuple-element.48.b_ref.j_ref, bf16[32,48,1024]{2,1,0:T(8,128)(2,1)} %all-to-all-done.x_ref.t_ref, bf16[32,48,1152]{2,1,0:T(8,128)(2,1)S(1)} %all-to-all-done.1.x_ref), custom_call_target="tpu_custom_call" | custom-call | flops 3774873600 | bytes 14024704 | tf_op jit(solution)/shard_map/pallas_call | solution.py:166
  168.3 2.7 copy-done
  173.0 2.2 copy-done.20
  175.2 3.3 %shard_map.123 = bf16[32,48,1024]{2,1,0:T(8,128)(2,1)S(1)} custom-call(bf16[32,48,256]{2,1,0:T(8,128)(2,1)S(1)} %copy-done.13, bf16[16,128,1024]{2,1,0:T(8,128)(2,1)S(1)} %copy-done.20), custom_call_target="tpu_custom_call" | custom-call | flops 2415919104 | bytes 8126464 | tf_op jit(solution)/shard_map/pallas_call | solution.py:166
  178.5 43.5 %all_to_all.20.m_ref = bf16[32,48,1024]{2,1,0:T(8,128)(2,1)} all-to-all(bf16[32,48,1024]{2,1,0:T(8,128)(2,1)S(1)} %shard_map.123), channel_id=1, replica_groups=mesh['y'=4,'c'=2,'x'=4,'z'=8] {'y','c','x'}, dimensions={0} | all-to-all | bytes 6291456 | tf_op jit(solution)/shard_map/all_to_all | solution.py:426
  222.0 6.6 %all-to-all-start.2 = ((bf16[32,48,1152]{2,1,0:T(8,128)(2,1)}), bf16[32,48,1152]{2,1,0:T(8,128)(2,1)}, u32[]{:S(2)}, u32[]{:S(2)}) async-start(bf16[32,48,1152]{2,1,0:T(8,128)(2,1)} %get-tuple-element.45), calls=%async_computation.2 | async-start | bytes 7077888 | tf_op jit(solution)/shard_map/all_to_all | solution.py:426
  228.9 1.9 copy-done.3
  230.8 2.5 shard_map.124
  233.3 38.7 %all-to-all-done.2.m_ref = bf16[32,48,1152]{2,1,0:T(8,128)(2,1)} async-done(((bf16[32,48,1152]{2,1,0:T(8,128)(2,1)}), bf16[32,48,1152]{2,1,0:T(8,128)(2,1)}, u32[]{:S(2)}, u32[]{:S(2)}) %all-to-all-start.2) | async-done | bytes 3538976 | tf_op jit(solution)/shard_map/all_to_all | solution.py:426
  272.9 4.6 %shard_map.122 = (bf16[128,8192]{1,0:T(8,128)(2,1)}, bf16[128,1024]{1,0:T(8,128)(2,1)}) custom-call(bf16[128,192]{1,0:T(8,128)(2,1)S(1)} %copy-done.15, bf16[32,48,1152]{2,1,0:T(8,128)(2,1)} %all-to-all-done.2.m_ref), custom_call_target="tpu_custom_call" | custom-call | flops 452984832 | bytes 5898240 | tf_op jit(solution)/shard_map/pallas_call | solution.py:140
  (90 shorter events, 39.1 us)
Async XLA Ops:
  7.2 67.3 %all-gather.5.cloned.1.call-start = ((), (), s32[]{:S(2)}) async-start(), calls=%async_computation.6 | async-start | bytes 2654208 | tf_op jit(solution)/shard_map/all_gather | solution.py:430
  8.9 104.3 %all-gather.3.cloned.1.call-start = ((), (), s32[]{:S(2)}) async-start(), calls=%async_computation.5 | async-start | bytes 4718592 | tf_op jit(solution)/shard_map/all_gather | solution.py:430
  18.1 51.1 %all-to-all-start.1 = ((bf16[32,48,1152]{2,1,0:T(8,128)(2,1)}), bf16[32,48,1152]{2,1,0:T(8,128)(2,1)S(1)}, u32[]{:S(2)}, u32[]{:S(2)}) async-start(bf16[32,48,1152]{2,1,0:T(8,128)(2,1)} %copy-done.1), calls=%async_computation.1 | async-start | bytes 7077888 | tf_op jit(solution)/shard_map/all_to_all | solution.py:426
  69.2 44.0 %all-to-all-start = ((bf16[32,48,1024]{2,1,0:T(8,128)(2,1)}), bf16[32,48,1024]{2,1,0:T(8,128)(2,1)}, u32[]{:S(2)}, u32[]{:S(2)}) async-start(bf16[32,48,1024]{2,1,0:T(8,128)(2,1)} %copy-done.2), calls=%async_computation | async-start | bytes 6291456 | tf_op jit(solution)/shard_map/all_to_all | solution.py:426
  74.4 203.1 %reduce-scatter.2.cloned.1.call-start = ((), (), s32[]{:S(2)}) async-start(), calls=%async_computation.7 | async-start | bytes 7372800 | tf_op jit(solution)/shard_map/reduce_scatter | solution.py:434
  82.1 38.2 %collective-permute-start.7 = (f32[4,48,128]{2,1,0:T(8,128)}, f32[4,48,128]{2,1,0:T(8,128)}, u32[]{:S(2)}, u32[]{:S(2)}) collective-permute-start(f32[4,48,128]{2,1,0:T(8,128)} %get-tuple-element.38), channel_id=1, source_target_pairs={{0,32},{32,0},{64,96},{96,64},{128,160},{160,128},{192,224},{224,1... | collective-permute-start | bytes 294920 | tf_op jit(solution)/shard_map/ppermute | solution.py:440
  82.5 38.5 %collective-permute-start.8 = (f32[4,48,128]{2,1,0:T(8,128)}, f32[4,48,128]{2,1,0:T(8,128)}, u32[]{:S(2)}, u32[]{:S(2)}) collective-permute-start(f32[4,48,128]{2,1,0:T(8,128)} %get-tuple-element.39), channel_id=1, source_target_pairs={{0,64},{32,96},{64,0},{96,32},{128,192},{160,224},{192,128},{224,1... | collective-permute-start | bytes 294920 | tf_op jit(solution)/shard_map/ppermute | solution.py:440
  83.6 37.9 %collective-permute-start.9 = (f32[4,48,128]{2,1,0:T(8,128)}, f32[4,48,128]{2,1,0:T(8,128)}, u32[]{:S(2)}, u32[]{:S(2)}) collective-permute-start(f32[4,48,128]{2,1,0:T(8,128)} %get-tuple-element.40), channel_id=1, source_target_pairs={{0,96},{32,64},{64,32},{96,0},{128,224},{160,192},{192,160},{224,1... | collective-permute-start | bytes 294920 | tf_op jit(solution)/shard_map/ppermute | solution.py:440
  84.3 39.2 %collective-permute-start.10 = (f32[4,48,128]{2,1,0:T(8,128)}, f32[4,48,128]{2,1,0:T(8,128)}, u32[]{:S(2)}, u32[]{:S(2)}) collective-permute-start(f32[4,48,128]{2,1,0:T(8,128)} %get-tuple-element.41), channel_id=1, source_target_pairs={{0,128},{32,160},{64,192},{96,224},{128,0},{160,32},{192,64},{224,... | collective-permute-start | bytes 294920 | tf_op jit(solution)/shard_map/ppermute | solution.py:440
  87.0 36.5 %collective-permute-start.11 = (f32[4,48,128]{2,1,0:T(8,128)}, f32[4,48,128]{2,1,0:T(8,128)}, u32[]{:S(2)}, u32[]{:S(2)}) collective-permute-start(f32[4,48,128]{2,1,0:T(8,128)} %get-tuple-element.42), channel_id=1, source_target_pairs={{0,160},{32,128},{64,224},{96,192},{128,32},{160,0},{192,96},{224,... | collective-permute-start | bytes 294920 | tf_op jit(solution)/shard_map/ppermute | solution.py:440
  115.4 4.9 %copy-start.24 = (f32[4,48,128]{2,1,0:T(8,128)S(1)}, f32[4,48,128]{2,1,0:T(8,128)}, u32[]{:S(2)}) copy-start(f32[4,48,128]{2,1,0:T(8,128)} %copy-done.23) | copy-start | bytes 294916
  115.4 5.6 %copy-start.22 = (f32[4,48,128]{2,1,0:T(8,128)S(1)}, f32[4,48,128]{2,1,0:T(8,128)}, u32[]{:S(2)}) copy-start(f32[4,48,128]{2,1,0:T(8,128)} %copy-done.21) | copy-start | bytes 294916
  115.4 23.7 %copy-start.18 = (f32[4,48,128]{2,1,0:T(8,128)S(1)}, f32[4,48,128]{2,1,0:T(8,128)}, u32[]{:S(2)}) copy-start(f32[4,48,128]{2,1,0:T(8,128)} %copy-done.17) | copy-start | bytes 294916
  115.4 42.2 %copy-start.5 = (bf16[16,64,1152]{2,1,0:T(8,128)(2,1)S(1)}, bf16[16,64,1152]{2,1,0:T(8,128)(2,1)}, u32[]{:S(2)}) copy-start(bf16[16,64,1152]{2,1,0:T(8,128)(2,1)} %all-gather.5.cloned.1.call-done.w_ref.refs_8_) | copy-start | bytes 7077892
  120.3 4.9 %collective-permute-start.12 = (f32[4,48,128]{2,1,0:T(8,128)S(1)}, f32[4,48,128]{2,1,0:T(8,128)S(1)}, u32[]{:S(2)}, u32[]{:S(2)}) collective-permute-start(f32[4,48,128]{2,1,0:T(8,128)S(1)} %copy-done.24), channel_id=1, source_target_pairs={{0,192},{32,224},{64,128},{96,160},{128,64},{160,96},{192,0},{224,... | collective-permute-start | bytes 294920 | tf_op jit(solution)/shard_map/ppermute | solution.py:440
  121.0 6.3 %collective-permute-start.13 = (f32[4,48,128]{2,1,0:T(8,128)S(1)}, f32[4,48,128]{2,1,0:T(8,128)S(1)}, u32[]{:S(2)}, u32[]{:S(2)}) collective-permute-start(f32[4,48,128]{2,1,0:T(8,128)S(1)} %copy-done.22), channel_id=1, source_target_pairs={{0,224},{32,192},{64,160},{96,128},{128,96},{160,64},{192,32},{224... | collective-permute-start | bytes 294920 | tf_op jit(solution)/shard_map/ppermute | solution.py:440
  121.6 6.9 %collective-permute-start = (f32[4,48,128]{2,1,0:T(8,128)S(1)}, f32[4,48,128]{2,1,0:T(8,128)S(1)}, u32[]{:S(2)}, u32[]{:S(2)}) collective-permute-start(f32[4,48,128]{2,1,0:T(8,128)S(1)} %get-tuple-element.30), channel_id=1, source_target_pairs={{0,32},{32,0},{64,96},{96,64},{128,160},{160,128},{192,224},{224,1... | collective-permute-start | bytes 294920 | tf_op jit(solution)/shard_map/ppermute | solution.py:440
  123.5 6.8 %collective-permute-start.1 = (f32[4,48,128]{2,1,0:T(8,128)S(1)}, f32[4,48,128]{2,1,0:T(8,128)S(1)}, u32[]{:S(2)}, u32[]{:S(2)}) collective-permute-start(f32[4,48,128]{2,1,0:T(8,128)S(1)} %get-tuple-element.31), channel_id=1, source_target_pairs={{0,64},{32,96},{64,0},{96,32},{128,192},{160,224},{192,128},{224,1... | collective-permute-start | bytes 294920 | tf_op jit(solution)/shard_map/ppermute | solution.py:440
  123.5 7.9 %collective-permute-start.2 = (f32[4,48,128]{2,1,0:T(8,128)S(1)}, f32[4,48,128]{2,1,0:T(8,128)S(1)}, u32[]{:S(2)}, u32[]{:S(2)}) collective-permute-start(f32[4,48,128]{2,1,0:T(8,128)S(1)} %get-tuple-element.32), channel_id=1, source_target_pairs={{0,96},{32,64},{64,32},{96,0},{128,224},{160,192},{192,160},{224,1... | collective-permute-start | bytes 294920 | tf_op jit(solution)/shard_map/ppermute | solution.py:440
  125.2 7.1 %collective-permute-start.3 = (f32[4,48,128]{2,1,0:T(8,128)S(1)}, f32[4,48,128]{2,1,0:T(8,128)S(1)}, u32[]{:S(2)}, u32[]{:S(2)}) collective-permute-start(f32[4,48,128]{2,1,0:T(8,128)S(1)} %get-tuple-element.33), channel_id=1, source_target_pairs={{0,128},{32,160},{64,192},{96,224},{128,0},{160,32},{192,64},{224,... | collective-permute-start | bytes 294920 | tf_op jit(solution)/shard_map/ppermute | solution.py:440
  127.3 7.4 %collective-permute-start.4 = (f32[4,48,128]{2,1,0:T(8,128)S(1)}, f32[4,48,128]{2,1,0:T(8,128)S(1)}, u32[]{:S(2)}, u32[]{:S(2)}) collective-permute-start(f32[4,48,128]{2,1,0:T(8,128)S(1)} %get-tuple-element.34), channel_id=1, source_target_pairs={{0,160},{32,128},{64,224},{96,192},{128,32},{160,0},{192,96},{224,... | collective-permute-start | bytes 294920 | tf_op jit(solution)/shard_map/ppermute | solution.py:440
  128.5 8.5 %collective-permute-start.5 = (f32[4,48,128]{2,1,0:T(8,128)S(1)}, f32[4,48,128]{2,1,0:T(8,128)S(1)}, u32[]{:S(2)}, u32[]{:S(2)}) collective-permute-start(f32[4,48,128]{2,1,0:T(8,128)S(1)} %get-tuple-element.35), channel_id=1, source_target_pairs={{0,192},{32,224},{64,128},{96,160},{128,64},{160,96},{192,0},{224,... | collective-permute-start | bytes 294920 | tf_op jit(solution)/shard_map/ppermute | solution.py:440
  130.2 8.8 %collective-permute-start.6 = (f32[4,48,128]{2,1,0:T(8,128)S(1)}, f32[4,48,128]{2,1,0:T(8,128)S(1)}, u32[]{:S(2)}, u32[]{:S(2)}) collective-permute-start(f32[4,48,128]{2,1,0:T(8,128)S(1)} %get-tuple-element.36), channel_id=1, source_target_pairs={{0,224},{32,192},{64,160},{96,128},{128,96},{160,64},{192,32},{224... | collective-permute-start | bytes 294920 | tf_op jit(solution)/shard_map/ppermute | solution.py:440
  140.2 5.7 %collective-permute-start.14 = (bf16[4,48,256]{2,1,0:T(8,128)(2,1)S(1)}, bf16[4,48,256]{2,1,0:T(8,128)(2,1)S(1)}, u32[]{:S(2)}, u32[]{:S(2)}) collective-permute-start(bf16[4,48,256]{2,1,0:T(8,128)(2,1)S(1)} %join_sums.1.refs_0_), channel_id=1, source_target_pairs={{0,32},{32,0},{64,96},{96,64},{128,160},{160,128},{192,224},{224,1... | collective-permute-start | bytes 294920 | tf_op jit(solution)/shard_map/ppermute | solution.py:440
  140.9 7.1 %collective-permute-start.15 = (bf16[4,48,256]{2,1,0:T(8,128)(2,1)S(1)}, bf16[4,48,256]{2,1,0:T(8,128)(2,1)S(1)}, u32[]{:S(2)}, u32[]{:S(2)}) collective-permute-start(bf16[4,48,256]{2,1,0:T(8,128)(2,1)S(1)} %join_sums.1.refs_0_), channel_id=1, source_target_pairs={{0,64},{32,96},{64,0},{96,32},{128,192},{160,224},{192,128},{224,1... | collective-permute-start | bytes 294920 | tf_op jit(solution)/shard_map/ppermute | solution.py:440
  140.9 8.0 %collective-permute-start.16 = (bf16[4,48,256]{2,1,0:T(8,128)(2,1)S(1)}, bf16[4,48,256]{2,1,0:T(8,128)(2,1)S(1)}, u32[]{:S(2)}, u32[]{:S(2)}) collective-permute-start(bf16[4,48,256]{2,1,0:T(8,128)(2,1)S(1)} %join_sums.1.refs_0_), channel_id=1, source_target_pairs={{0,96},{32,64},{64,32},{96,0},{128,224},{160,192},{192,160},{224,1... | collective-permute-start | bytes 294920 | tf_op jit(solution)/shard_map/ppermute | solution.py:440
  142.7 8.5 %collective-permute-start.17 = (bf16[4,48,256]{2,1,0:T(8,128)(2,1)S(1)}, bf16[4,48,256]{2,1,0:T(8,128)(2,1)S(1)}, u32[]{:S(2)}, u32[]{:S(2)}) collective-permute-start(bf16[4,48,256]{2,1,0:T(8,128)(2,1)S(1)} %join_sums.1.refs_0_), channel_id=1, source_target_pairs={{0,128},{32,160},{64,192},{96,224},{128,0},{160,32},{192,64},{224,... | collective-permute-start | bytes 294920 | tf_op jit(solution)/shard_map/ppermute | solution.py:440
  144.2 9.4 %collective-permute-start.18 = (bf16[4,48,256]{2,1,0:T(8,128)(2,1)S(1)}, bf16[4,48,256]{2,1,0:T(8,128)(2,1)S(1)}, u32[]{:S(2)}, u32[]{:S(2)}) collective-permute-start(bf16[4,48,256]{2,1,0:T(8,128)(2,1)S(1)} %join_sums.1.refs_0_), channel_id=1, source_target_pairs={{0,160},{32,128},{64,224},{96,192},{128,32},{160,0},{192,96},{224,... | collective-permute-start | bytes 294920 | tf_op jit(solution)/shard_map/ppermute | solution.py:440
  145.9 9.6 %collective-permute-start.19 = (bf16[4,48,256]{2,1,0:T(8,128)(2,1)S(1)}, bf16[4,48,256]{2,1,0:T(8,128)(2,1)S(1)}, u32[]{:S(2)}, u32[]{:S(2)}) collective-permute-start(bf16[4,48,256]{2,1,0:T(8,128)(2,1)S(1)} %join_sums.1.refs_0_), channel_id=1, source_target_pairs={{0,192},{32,224},{64,128},{96,160},{128,64},{160,96},{192,0},{224,... | collective-permute-start | bytes 294920 | tf_op jit(solution)/shard_map/ppermute | solution.py:440
  148.0 9.6 %collective-permute-start.20 = (bf16[4,48,256]{2,1,0:T(8,128)(2,1)S(1)}, bf16[4,48,256]{2,1,0:T(8,128)(2,1)S(1)}, u32[]{:S(2)}, u32[]{:S(2)}) collective-permute-start(bf16[4,48,256]{2,1,0:T(8,128)(2,1)S(1)} %join_sums.1.refs_0_), channel_id=1, source_target_pairs={{0,224},{32,192},{64,160},{96,128},{128,96},{160,64},{192,32},{224... | collective-permute-start | bytes 294920 | tf_op jit(solution)/shard_map/ppermute | solution.py:440
  222.0 6.6 %copy-start.10 = (s32[128,1]{1,0:T(8,128)S(1)}, s32[128,1]{1,0:T(8,128)}, u32[]{:S(2)}) copy-start(s32[128,1]{1,0:T(8,128)} %copy.16.a_ref) | copy-start | bytes 1540
  222.0 50.0 %all-to-all-start.2 = ((bf16[32,48,1152]{2,1,0:T(8,128)(2,1)}), bf16[32,48,1152]{2,1,0:T(8,128)(2,1)}, u32[]{:S(2)}, u32[]{:S(2)}) async-start(bf16[32,48,1152]{2,1,0:T(8,128)(2,1)} %get-tuple-element.45), calls=%async_computation.2 | async-start | bytes 7077888 | tf_op jit(solution)/shard_map/all_to_all | solution.py:426
  (20 other events, 28.4 us)
Sparse Core Ops, SparseCore 0:
  10.3 40.4 all-gather.4
  52.6 56.9 all-gather.2
  172.0 78.4 reduce-scatter.1
